TPU v7x, 32 devices: a whole 2x2x4 slice. The times are simulated.
32 devices in a mesh: tm: 4 (over y, x), rows: 2 (over core), cols: 4 (over z).
Axes of the slice: x: 2, y: 2, z: 4, core: 2. Of those that a mesh axis runs over, the one named last changes fastest.
Arguments:
- inputs: bfloat16 [4, 34, 32, 128], P('tm', 'rows', 'cols'), may hold values from -6 to 6
- cotangent: bfloat16 [4, 34, 32, 128], P('tm', 'rows', 'cols'), may hold values from -6 to 6
- weight_one: bfloat16 [27, 128, 128], replicated, may hold values from -0.109375 to 0.109375
- weight_two: bfloat16 [27, 128, 128], replicated, may hold values from -0.109375 to 0.109375
Outputs:
- grad_inputs: float32 [4, 34, 32, 128], P('tm', 'rows', 'cols')
- grad_one: float32 [27, 128, 128], P(None, ('tm', 'rows'), 'cols')
- grad_two: float32 [27, 128, 128], P(None, ('tm', 'rows'), 'cols')
All inputs are finite; a program needn't handle non-finite values.
Results may differ from a plain program's by a relative error of at most 0.0029.
Values may be sent and summed in bfloat16 or wider, within the bound.
A program may use at most 64 MiB of HBM per device.

v0:
```python
import functools

import jax
import jax.numpy as jnp
from jax import lax
from jax.experimental import pallas as pl
from jax.experimental.pallas import tpu as pltpu
from jax.sharding import PartitionSpec as P

MESH = pl.DeviceIdType.MESH
NT = (((1,), (1,)), ((), ()))


def kernel(
    dims,
    x_ref,
    c_ref,
    w1_ref,
    w2_ref,
    back_ref,
    acc,
    flat,
    edge,
    w1v,
    hid,
    gat,
    hal,
    sx,
    sg,
    sh,
    sa,
    imc,
    w1r,
    w2r,
    lt,
    pp,
    edges_out,
    edges_in,
    stage,
    landed,
    own_sem,
    w1_sem,
    w2_sem,
    blk_send,
    blk_recv,
    edge_send,
    edge_recv,
    hal_send,
    hal_recv,
    gh_send,
    gh_recv,
    rs_send,
    rs_recv,
):
    tmn, rn, zn, rows, cols, chunk, chunk_pad, slots = dims
    plane = tmn * rn
    height = rn * rows
    pitch = (height + 2) * cols
    cells = rows * cols
    frame_cells = height * cols
    span = tmn * pitch
    ochunk = 128 // zn
    tm, row, col = lax.axis_index("tm"), lax.axis_index("rows"), lax.axis_index("cols")
    me = tm * rn + row

    def place(index, z):
        return (index // rn, lax.rem(index, rn), z)

    has_low, has_high = col > 0, col < zn - 1

    barrier = pltpu.get_barrier_semaphore()

    def greet(index, z):
        pl.semaphore_signal(barrier, inc=1, device_id=place(index, z), device_id_type=MESH)

    for d in range(1, plane):
        greet(lax.rem(me + d, plane), col)

    for step in range(1, zn):
        greet(me, lax.rem(col + step, zn))

    blocks = (x_ref, c_ref)

    def keep(which):
        return pltpu.make_async_copy(blocks[which], gat.at[which, me], own_sem.at[which])

    def load_two(k):
        part = pl.ds(128 * k, 128)
        return pltpu.make_async_copy(w2_ref.at[part, :], w2r.at[:, part], w2_sem.at[k])

    load_one = pltpu.make_async_copy(w1_ref, w1v, w1_sem)
    keep(0).start()
    keep(1).start()
    load_one.start()
    for k in range(27):
        load_two(k).start()

    def blank(dst, lead):
        if lead:
            dst[:lead, :] = jnp.zeros((lead, 128), jnp.float32)
        for f in range(tmn):
            at = lead + f * pitch
            dst[at : at + cols, :] = jnp.zeros((cols, 128), jnp.float32)
            dst[at + pitch - cols : at + pitch, :] = jnp.zeros((cols, 128), jnp.float32)
        at = lead + span
        dst[at:, :] = jnp.zeros((dst.shape[0] - at, 128), jnp.float32)

    for e in range(3):
        blank(sx.at[e], 2 * pitch)
    for which in range(2):
        keep(which).wait()
        flat[...] = gat[which, me].astype(jnp.float32)
        for side in range(2):
            edge[side, which] = flat[pl.ds(side * (cols - 1), rows, stride=cols), :].astype(jnp.bfloat16)

    @pl.when(col == 0)
    def _():
        hal[me, 0] = jnp.zeros((2, rows, 128), jnp.bfloat16)

    @pl.when(col == zn - 1)
    def _():
        hal[me, 1] = jnp.zeros((2, rows, 128), jnp.bfloat16)

    pl.semaphore_wait(barrier, plane - 1 + zn - 1)

    def send_block(which, d):
        peer = lax.rem(me + d, plane)
        return pltpu.make_async_remote_copy(
            src_ref=gat.at[which, me],
            dst_ref=gat.at[which, me],
            send_sem=blk_send.at[which, d],
            recv_sem=blk_recv.at[which, me],
            device_id=place(peer, col),
            device_id_type=MESH,
        )

    def send_rim(side):
        return pltpu.make_async_remote_copy(
            src_ref=edge.at[side],
            dst_ref=hal.at[me, 1 - side],
            send_sem=edge_send.at[side],
            recv_sem=edge_recv.at[1 - side],
            device_id=place(me, col - 1 if side == 0 else col + 1),
            device_id_type=MESH,
        )

    def send_halo(d):
        return pltpu.make_async_remote_copy(
            src_ref=hal.at[me],
            dst_ref=hal.at[me],
            send_sem=hal_send.at[d],
            recv_sem=hal_recv.at[me],
            device_id=place(lax.rem(me + d, plane), col),
            device_id_type=MESH,
        )

    @pl.when(has_low)
    def _():
        send_rim(0).start()

    @pl.when(has_high)
    def _():
        send_rim(1).start()

    for d in range(1, plane):
        send_block(0, d).start()

    for e in range(3):
        blank(sg.at[e], 0)
    blank(sh.at[1], 0)
    for e in (0, 2):
        sh[e, span:, :] = jnp.zeros((sh.shape[1] - span, 128), jnp.float32)
    blank(sa, 2 * pitch)
    pp[27 * chunk_pad :, :] = jnp.zeros((pp.shape[0] - 27 * chunk_pad, 128), jnp.float32)

    def arrived(dst, sem, z):
        pltpu.make_async_remote_copy(
            src_ref=dst, dst_ref=dst, send_sem=sem, recv_sem=sem,
            device_id=place(me, z), device_id_type=MESH,
        ).wait_recv()

    @pl.when(has_low)
    def _():
        arrived(hal.at[me, 0], edge_recv.at[0], col - 1)

    @pl.when(has_high)
    def _():
        arrived(hal.at[me, 1], edge_recv.at[1], col + 1)

    for d in range(1, plane):
        send_halo(d).start()
    for d in range(1, plane):
        send_block(1, d).start()

    load_one.wait()
    for k in range(27):
        w1r[:, 128 * k : 128 * (k + 1)] = w1v[128 * k : 128 * (k + 1), :]

    def gather(which, dst, ahead):
        for m in range(plane):

            @pl.when(me != m)
            def _():
                arrived(gat.at[which, m], blk_recv.at[which, m], col)
                if which == 0:
                    arrived(hal.at[m], hal_recv.at[m], col)

            base = (m // rn + ahead) * pitch + (m % rn * rows + 1) * cols
            v = gat[which, m].astype(jnp.float32)
            dst[1, base : base + cells] = v
            dst[0, base + 1 : base + cells] = v[: cells - 1]
            dst[2, base : base + cells - 1] = v[1:]
            dst[0, pl.ds(base, rows, stride=cols), :] = hal[m, 0, which].astype(jnp.float32)
            dst[2, pl.ds(base + cols - 1, rows, stride=cols), :] = hal[m, 1, which].astype(jnp.float32)

    def past(src, base, count):
        for k in range(27):
            a, b, e = k // 9, k // 3 % 3, k % 3
            at = pl.multiple_of(base + a * pitch + b * cols, 8)
            imc[:count, 128 * k : 128 * (k + 1)] = src[e, pl.ds(at, count), :].astype(jnp.bfloat16)

    def future(src, base, count):
        for k in range(27):
            a, b, e = k // 9, k // 3 % 3, k % 3
            at = pl.multiple_of(base + (2 - a) * pitch + (2 - b) * cols, 8)
            imc[:count, 128 * k : 128 * (k + 1)] = src[2 - e, pl.ds(at, count), :].astype(jnp.bfloat16)

    group = slots * chunk_pad // zn
    taps = 27 * chunk_pad
    picked = jnp.where(
        (lax.broadcasted_iota(jnp.int32, (chunk_pad, 128), 1)
         == me * chunk + lax.broadcasted_iota(jnp.int32, (chunk_pad, 128), 0))
        & (lax.broadcasted_iota(jnp.int32, (chunk_pad, 128), 0) < chunk),
        1.0, 0.0,
    ).astype(jnp.bfloat16)

    def tall(src):
        return lax.dot_general(picked, src.astype(jnp.bfloat16), NT, preferred_element_type=jnp.float32)

    def send_piece(tensor, z):
        return pltpu.make_async_remote_copy(
            src_ref=stage.at[tensor, z],
            dst_ref=landed.at[tensor, col],
            send_sem=rs_send.at[tensor, z],
            recv_sem=rs_recv.at[tensor, col],
            device_id=place(me, z),
            device_id_type=MESH,
        )

    def scatter(tensor):
        for z in range(zn):
            stage[tensor, z] = jnp.concatenate(
                [pp[group * q : group * (q + 1), ochunk * z : ochunk * (z + 1)] for q in range(zn)],
                axis=1,
            ).astype(jnp.bfloat16)
        for z in range(zn):

            @pl.when(col != z)
            def _():
                send_piece(tensor, z).start()

    gather(0, sx, 2)

    def forward_step(t, carry):
        base = pl.multiple_of(t * pitch, 8)
        past(sx, base, frame_cells)
        hidden = jnp.dot(imc[:frame_cells, :], w1v[...], preferred_element_type=jnp.float32)
        hid[t] = hidden
        activation = (hidden * jax.nn.sigmoid(hidden)).astype(jnp.bfloat16)
        at = pl.multiple_of(base + cols + 2 * pitch, 8)
        sa[pl.ds(at, frame_cells), :] = activation.astype(jnp.float32)
        return carry

    lax.fori_loop(0, tmn, forward_step, 0)

    gather(1, sg, 0)
    at = tall(sa[...])
    for ab in range(9):
        off = ab // 3 * pitch + ab % 3 * cols
        lt[ab * chunk_pad : (ab + 1) * chunk_pad, :] = at[:, off : off + span].astype(jnp.bfloat16)
    for e in range(3):
        part = jnp.dot(
            lt[: 9 * chunk_pad, :], sg[2 - e, cols : cols + span, :].astype(jnp.bfloat16),
            preferred_element_type=jnp.float32,
        )
        for ab in range(9):
            k = 3 * ab + e
            pp[k * chunk_pad : (k + 1) * chunk_pad, :] = part[ab * chunk_pad : (ab + 1) * chunk_pad]
    scatter(1)

    for k in range(27):
        load_two(k).wait()

    def backward_step(t, carry):
        base = pl.multiple_of(t * pitch, 8)
        future(sg, base, frame_cells)
        grad_act = lax.dot_general(
            imc[:frame_cells, :], w2r[...], NT, preferred_element_type=jnp.float32
        )
        hidden = hid[t]
        squash = jax.nn.sigmoid(hidden)
        grad_hidden = (grad_act * squash * (1.0 + hidden * (1.0 - squash))).astype(jnp.bfloat16)
        at = pl.multiple_of(base + cols, 8)
        sh[1, pl.ds(at, frame_cells), :] = grad_hidden.astype(jnp.float32)
        return carry

    lax.fori_loop(0, tmn, backward_step, 0)

    lines = tmn * (height + 2)
    edges_out[0] = sh[1, pl.ds(0, lines, stride=cols), :].astype(jnp.bfloat16)
    edges_out[1] = sh[1, pl.ds(cols - 1, lines, stride=cols), :].astype(jnp.bfloat16)

    def send_edge(side):
        return pltpu.make_async_remote_copy(
            src_ref=edges_out.at[side],
            dst_ref=edges_in.at[1 - side],
            send_sem=gh_send.at[side],
            recv_sem=gh_recv.at[1 - side],
            device_id=place(me, col - 1 if side == 0 else col + 1),
            device_id_type=MESH,
        )

    @pl.when(has_low)
    def _():
        send_edge(0).start()

    @pl.when(has_high)
    def _():
        send_edge(1).start()

    for e in range(3):
        xt = tall(sx[e])
        for ab in range(9):
            off = ab // 3 * pitch + ab % 3 * cols
            k = 3 * ab + e
            lt[k * chunk_pad : (k + 1) * chunk_pad, :] = xt[:, off : off + span].astype(jnp.bfloat16)
    pp[:taps, :] = jnp.dot(
        lt[:taps, :], sh[1, cols : cols + span, :].astype(jnp.bfloat16),
        preferred_element_type=jnp.float32,
    )
    scatter(0)

    sh[0, 1 : span, :] = sh[1, : span - 1, :]
    sh[2, : span - 1, :] = sh[1, 1:span, :]
    nothing = jnp.zeros((lines, 128), jnp.float32)
    sh[0, pl.ds(0, lines, stride=cols), :] = nothing
    sh[2, pl.ds(cols - 1, lines, stride=cols), :] = nothing

    @pl.when(has_low)
    def _():
        arrived(edges_in.at[0], gh_recv.at[0], col - 1)
        sh[0, pl.ds(0, lines, stride=cols), :] = edges_in[0].astype(jnp.float32)

    @pl.when(has_high)
    def _():
        arrived(edges_in.at[1], gh_recv.at[1], col + 1)
        sh[2, pl.ds(cols - 1, lines, stride=cols), :] = edges_in[1].astype(jnp.float32)

    future(sh, pl.multiple_of(tm * pitch + row * cells, 8), cells)
    back_ref[...] = gat[1, me].astype(jnp.float32) + lax.dot_general(
        imc[:cells, :], w1r[...], NT, preferred_element_type=jnp.float32
    )

    for tensor in (1, 0):
        acc[tensor] = stage[tensor, col].astype(jnp.float32)
        for z in range(zn):

            @pl.when(col != z)
            def _():
                arrived(landed.at[tensor, z], rs_recv.at[tensor, z], z)
                acc[tensor] += landed[tensor, z].astype(jnp.float32)

    for which in range(2):
        for d in range(1, plane):
            send_block(which, d).wait_send()
        for z in range(zn):

            @pl.when(col != z)
            def _():
                send_piece(which, z).wait_send()

    for d in range(1, plane):
        send_halo(d).wait_send()

    @pl.when(has_low)
    def _():
        send_rim(0).wait_send()
        send_edge(0).wait_send()

    @pl.when(has_high)
    def _():
        send_rim(1).wait_send()
        send_edge(1).wait_send()


def finish(zn, chunk, chunk_pad, slots, back_ref, acc_ref, out_ref, one_ref, two_ref):
    ochunk = 128 // zn
    out_ref[...] = back_ref[...]
    for tensor, out in enumerate((one_ref, two_ref)):
        got = acc_ref[tensor]
        whole = jnp.concatenate(
            [got[:, ochunk * q : ochunk * (q + 1)] for q in range(zn)], axis=0
        ).reshape(slots, chunk_pad, ochunk)
        out[...] = whole[:27, :chunk, :]


def body(sizes, inputs, cotangent, weight_one, weight_two):
    tmn, rn, zn = sizes
    _, rows, cols, channels = inputs.shape
    plane = tmn * rn
    cells = rows * cols
    chunk = channels // plane
    chunk_pad = max(16, chunk)
    slots = 28
    pitch = (rn * rows + 2) * cols
    total = -(-((tmn + 2) * pitch + 2 * cols) // 128) * 128
    dims = (tmn, rn, zn, rows, cols, chunk, chunk_pad, slots)
    vmem = pl.BlockSpec(memory_space=pltpu.VMEM)
    bf, f32 = jnp.bfloat16, jnp.float32
    group = slots * chunk_pad // zn
    lines = tmn * (rn * rows + 2)
    frame_cells = rn * rows * cols
    dma = pltpu.SemaphoreType.DMA
    back, acc = pl.pallas_call(
        functools.partial(kernel, dims),
        out_shape=(
            jax.ShapeDtypeStruct((cells, channels), f32),
            jax.ShapeDtypeStruct((2, group, channels), f32),
        ),
        in_specs=[pl.BlockSpec(memory_space=pl.ANY)] * 4,
        out_specs=(vmem,) * 2,
        scratch_shapes=[
            pltpu.VMEM((cells, channels), f32),
            pltpu.VMEM((2, 2, rows, channels), bf),
            pltpu.VMEM((27 * channels, channels), bf),
            pltpu.VMEM((tmn, frame_cells, channels), f32),
            pltpu.VMEM((2, plane, cells, channels), bf),
            pltpu.VMEM((plane, 2, 2, rows, channels), bf),
            pltpu.VMEM((3, total, channels), f32),
            pltpu.VMEM((3, total, channels), f32),
            pltpu.VMEM((3, total, channels), f32),
            pltpu.VMEM((total, channels), f32),
            pltpu.VMEM((frame_cells, 27 * channels), bf),
            pltpu.VMEM((channels, 27 * channels), bf),
            pltpu.VMEM((channels, 27 * channels), bf),
            pltpu.VMEM((slots * chunk_pad, tmn * pitch), bf),
            pltpu.VMEM((slots * chunk_pad, channels), f32),
            pltpu.VMEM((2, lines, channels), bf),
            pltpu.VMEM((2, lines, channels), bf),
            pltpu.VMEM((2, zn, group, channels), bf),
            pltpu.VMEM((2, zn, group, channels), bf),
            dma((2,)),
            dma,
            dma((27,)),
            dma((2, plane)),
            dma((2, plane)),
            dma((2,)),
            dma((2,)),
            dma((plane,)),
            dma((plane,)),
            dma((2,)),
            dma((2,)),
            dma((2, zn)),
            dma((2, zn)),
        ],
        compiler_params=pltpu.CompilerParams(
            collective_id=0, has_side_effects=True, vmem_limit_bytes=60 * 1024 * 1024
        ),
    )(
        inputs.reshape(cells, channels),
        cotangent.reshape(cells, channels),
        weight_one.reshape(27 * channels, channels),
        weight_two.reshape(27 * channels, channels),
    )
    back, one, two = pl.pallas_call(
        functools.partial(finish, zn, chunk, chunk_pad, slots),
        out_shape=(
            jax.ShapeDtypeStruct((cells, channels), f32),
            jax.ShapeDtypeStruct((27, chunk, channels // zn), f32),
            jax.ShapeDtypeStruct((27, chunk, channels // zn), f32),
        ),
        in_specs=[vmem] * 2,
        out_specs=(vmem,) * 3,
    )(back, acc)
    return back.reshape(1, rows, cols, channels), one, two


def solution(mesh):
    sizes = (mesh.shape["tm"], mesh.shape["rows"], mesh.shape["cols"])
    placed = (P("tm", "rows", "cols", None), P("tm", "rows", "cols", None), P(), P())
    return jax.shard_map(
        functools.partial(body, sizes),
        mesh=mesh,
        in_specs=placed,
        out_specs=(
            P("tm", "rows", "cols", None),
            P(None, ("tm", "rows"), "cols"),
            P(None, ("tm", "rows"), "cols"),
        ),
        check_vma=False,
    )
```

profile of v0, /device:TPU:0, one launch (start us, length us, event | category | flops | bytes accessed | tf_op | source)
XLA Modules:
  0.0 29.4 jit_solution(7423977465718805192)
XLA Ops:
  0.6 26.9 %shard_map.67 = (f32[136,128]{1,0:T(8,128)}, f32[2,112,128]{2,1,0:T(8,128)}) custom-call(bf16[136,128]{1,0:T(8,128)(2,1)} %bitcast.7, bf16[136,128]{1,0:T(8,128)(2,1)} %bitcast.8, bf16[3456,128]{1,0:T(8,128)(2,1)} %bitcast.5, bf16[3456,128]{1,0:T(8,128)(2,1)} %bitcast.6), custom_call_target="tpu_custom_call" | custom-call | tf_op jit(solution)/shard_map/pallas_call | solution.py:424
  27.5 1.8 %shard_map.68 = (f32[136,128]{1,0:T(8,128)}, f32[27,16,32]{2,1,0:T(8,128)}, f32[27,16,32]{2,1,0:T(8,128)}) custom-call(f32[136,128]{1,0:T(8,128)} %get-tuple-element.8.back_ref, f32[2,112,128]{2,1,0:T(8,128)} %get-tuple-element.9.acc_ref), custom_call_target="tpu_custom_call" | custom-call | tf_op jit(solution)/shard_map/pallas_call | solution.py:475
where the time goes:
time: 29.5 us; the launch traced here: 29.4 us
  Pallas kernels  28.7 us (97%)
  between operations  0.64 us (2%)
    pallas_call x1, Pallas kernels, body(): pl.pallas_call(functools.partial(kernel, dims), out_shape=(jax.ShapeDtype...  26.9 us
    pallas_call x1, Pallas kernels, body(): pl.pallas_call(functools.partial(finish, zn, chunk, chunk_pad, slots), ou...  1.8 us

commit v1 on v0

v1 whole, which is shorter than its diff:
```python
import functools

import jax
import jax.numpy as jnp
from jax import lax
from jax.experimental import pallas as pl
from jax.experimental.pallas import tpu as pltpu
from jax.sharding import PartitionSpec as P

MESH = pl.DeviceIdType.MESH
NT = (((1,), (1,)), ((), ()))
C = 128


def kernel(
    dims,
    x_ref,
    c_ref,
    w1_ref,
    w2_ref,
    back_ref,
    acc,
    gat,
    flat,
    hf,
    hal,
    sx,
    sc,
    x9,
    c9,
    r1,
    r2,
    conv,
    gate,
    at,
    xt,
    ghb,
    ghf,
    own3,
    gf,
    sh,
    imc,
    part,
    pstage,
    pland,
    pp,
    stage,
    landed,
    rim,
    edge,
    rim_in,
    edge_in,
    corner_in,
    grim,
    gedge,
    grim_in,
    gedge_in,
    gcorner_in,
    own_sem,
    w1_sem,
    w2_sem,
    blk_send,
    blk_recv,
    hal_send,
    hal_recv,
    near_sem,
    gnear_sem,
    pair_send,
    pair_recv,
    rs_send,
    rs_recv,
):
    tmn, rn, zn, rows, cols, chunk, chunk_pad, slots = dims
    cells = rows * cols
    lift = (rows + 2) * cols
    left = 2 * cols
    right = left + -(-(rows + 2) // 8) * 8
    mp, kp = x9.shape[1], c9.shape[1]
    taps = 27 * chunk_pad
    cwp = rn * chunk_pad
    ochunk = C // zn
    bf, f32 = jnp.bfloat16, jnp.float32
    tm, row, col = lax.axis_index("tm"), lax.axis_index("rows"), lax.axis_index("cols")
    vert = (row > 0, row < rn - 1)
    side = (col > 0, col < zn - 1)
    step = (-1, 1)

    barrier = pltpu.get_barrier_semaphore()

    def greet(place):
        pl.semaphore_signal(barrier, inc=1, device_id=place, device_id_type=MESH)

    for d in range(1, tmn):
        greet((lax.rem(tm + d, tmn), row, col))
    for d in range(1, rn):
        greet((tm, lax.rem(row + d, rn), col))
    for d in range(1, zn):
        greet((tm, row, lax.rem(col + d, zn)))
    for v in range(2):
        for h in range(2):

            @pl.when(jnp.logical_and(vert[v], side[h]))
            def _():
                greet((tm, row + step[v], col + step[h]))

    blocks = (x_ref, c_ref)

    def keep(which):
        return pltpu.make_async_copy(blocks[which], gat.at[which, tm], own_sem.at[which])

    def load_one(k):
        a, q = k // 9, k % 9
        return pltpu.make_async_copy(
            w1_ref.at[pl.ds(C * k, C), :], r1.at[pl.ds(C * q, C), pl.ds(C * a, C)], w1_sem.at[k]
        )

    def load_two(k):
        a, q = k // 9, k % 9
        return pltpu.make_async_copy(
            w2_ref.at[pl.ds(C * k, C), :], r2.at[pl.ds(C * a, C), pl.ds(C * q, C)], w2_sem.at[k]
        )

    keep(0).start()
    keep(1).start()
    for k in range(27):
        load_one(k).start()
    for k in range(27):
        load_two(k).start()

    hf[...] = jnp.zeros(hf.shape, f32)

    for which in range(2):
        keep(which).wait()
        flat[which] = gat[which, tm].astype(f32)
        for h in range(2):
            edge[h, which * rows : (which + 1) * rows, :] = flat[
                which, pl.ds(h * (cols - 1), rows, stride=cols), :
            ].astype(bf)
        for v in range(2):
            rim[v, which * cols : (which + 1) * cols, :] = flat[
                which, v * (cells - cols) : v * (cells - cols) + cols, :
            ].astype(bf)

    def remote(src, dst, send, recv, place):
        return pltpu.make_async_remote_copy(
            src_ref=src, dst_ref=dst, send_sem=send, recv_sem=recv, device_id=place, device_id_type=MESH
        )

    def near(out_rim, out_edge, in_rim, in_edge, in_corner, sems):
        found = []
        for v in range(2):
            found.append((
                vert[v],
                lambda v=v: remote(
                    out_rim.at[v], in_rim.at[1 - v], sems.at[0, v], sems.at[1, 1 - v], (tm, row + step[v], col)
                ),
                in_rim.at[v],
                sems.at[1, v],
            ))
        for h in range(2):
            found.append((
                side[h],
                lambda h=h: remote(
                    out_edge.at[h], in_edge.at[1 - h], sems.at[0, 2 + h], sems.at[1, 3 - h], (tm, row, col + step[h])
                ),
                in_edge.at[h],
                sems.at[1, 2 + h],
            ))
        for v in range(2):
            for h in range(2):
                found.append((
                    jnp.logical_and(vert[v], side[h]),
                    lambda v=v, h=h: remote(
                        out_edge.at[h],
                        in_corner.at[1 - v, 1 - h],
                        sems.at[0, 4 + 2 * v + h],
                        sems.at[1, 4 + 2 * (1 - v) + 1 - h],
                        (tm, row + step[v], col + step[h]),
                    ),
                    in_corner.at[v, h],
                    sems.at[1, 4 + 2 * v + h],
                ))
        return found

    def start_all(found):
        for cond, copy, _, _ in found:

            @pl.when(cond)
            def _():
                copy().start()

    def drain_all(found):
        for cond, copy, _, _ in found:

            @pl.when(cond)
            def _():
                copy().wait_send()

    def arrived(dst, sem):
        remote(dst, dst, sem, sem, (tm, row, col)).wait_recv()

    def await_all(found):
        for cond, _, dst, sem in found:

            @pl.when(cond)
            def _():
                arrived(dst, sem)

    def assemble(dst, count, in_rim, in_edge, in_corner):
        for v in range(2):

            @pl.when(vert[v])
            def _():
                got = in_rim[v].astype(f32)
                for q in range(count):
                    dst[q, v * cols : (v + 1) * cols, :] = got[q * cols : (q + 1) * cols]

        for h, base in enumerate((left, right)):

            @pl.when(side[h])
            def _():
                got = in_edge[h].astype(f32)
                for q in range(count):
                    dst[q, base + 1 : base + 1 + rows, :] = got[q * rows : (q + 1) * rows]

            for v in range(2):

                @pl.when(jnp.logical_and(vert[v], side[h]))
                def _():
                    got = in_corner[v, h].astype(f32)
                    put = base + v * (rows + 1)
                    for q in range(count):
                        take = q * rows + (1 - v) * (rows - 1)
                        dst[q, put : put + 1, :] = got[take : take + 1]

    def spread(dst, v, h):
        top, bottom = h[:cols], h[cols : 2 * cols]
        dst[1, :cols, :] = top
        dst[1, cols : cols + cells, :] = v
        dst[1, cols + cells : lift, :] = bottom
        dst[0, 1 : cols + 1, :] = top
        dst[0, cols + 1 : cols + cells + 1, :] = v
        dst[0, cols + cells + 1 : lift, :] = bottom[: cols - 1]
        dst[0, pl.ds(0, rows + 2, stride=cols), :] = h[left : left + rows + 2]
        dst[2, : cols - 1, :] = top[1:]
        dst[2, cols - 1 : cols + cells - 1, :] = v
        dst[2, cols + cells - 1 : lift - 1, :] = bottom
        dst[2, pl.ds(cols - 1, rows + 2, stride=cols), :] = h[right : right + rows + 2]

    corners = (vert[0].astype(jnp.int32) + vert[1].astype(jnp.int32)) * (
        side[0].astype(jnp.int32) + side[1].astype(jnp.int32)
    )
    pl.semaphore_wait(barrier, tmn + rn + zn - 3 + corners)

    rims = near(rim, edge, rim_in, edge_in, corner_in, near_sem)
    start_all(rims)

    def send_block(which, d):
        return remote(
            gat.at[which, tm],
            gat.at[which, tm],
            blk_send.at[which, d],
            blk_recv.at[which, tm],
            (lax.rem(tm + d, tmn), row, col),
        )

    def send_halo(d):
        return remote(
            hal.at[tm], hal.at[tm], hal_send.at[d], hal_recv.at[tm], (lax.rem(tm + d, tmn), row, col)
        )

    for d in range(1, tmn):
        send_block(0, d).start()

    for tail in (sx, sc):
        for s in range(tmn):
            for e in range(3):
                tail[s, e, lift:, :] = jnp.zeros((tail.shape[2] - lift, C), f32)
    for s in range(tmn):
        c9[s, mp:, :] = jnp.zeros((kp - mp, 9 * C), bf)
        xt[s] = jnp.zeros(xt.shape[1:], bf)
    at[...] = jnp.zeros(at.shape, bf)
    for s in range(tmn + 2):
        ghb[s] = jnp.zeros((kp, C), bf)
    ghf[tmn * cells :, :] = jnp.zeros((2 * cells, C), f32)
    gf[...] = jnp.zeros(gf.shape, f32)
    for j in range(3):
        for e in range(3):
            sh[j, e, lift:, :] = jnp.zeros((sh.shape[2] - lift, C), f32)
    pp[taps:, :] = jnp.zeros((pp.shape[0] - taps, C), f32)
    picked = jnp.concatenate(
        [
            jnp.where(
                (lax.broadcasted_iota(jnp.int32, (chunk_pad, C), 1)
                 == (tm * rn + r) * chunk + lax.broadcasted_iota(jnp.int32, (chunk_pad, C), 0))
                & (lax.broadcasted_iota(jnp.int32, (chunk_pad, C), 0) < chunk),
                1.0, 0.0,
            )
            for r in range(rn)
        ],
        axis=0,
    ).astype(bf)

    def tall(src):
        return lax.dot_general(picked, src, NT, preferred_element_type=f32).astype(bf)

    await_all(rims)
    assemble(hf, 2, rim_in, edge_in, corner_in)
    for which in range(2):
        hal[tm, which] = hf[which].astype(bf)
    for d in range(1, tmn):
        send_halo(d).start()
    for d in range(1, tmn):
        send_block(1, d).start()

    for m in range(tmn):

        @pl.when(tm != m)
        def _():
            arrived(gat.at[0, m], blk_recv.at[0, m])
            arrived(hal.at[m], hal_recv.at[m])

        spread(sx.at[m], gat[0, m].astype(f32), hal[m, 0].astype(f32))
        for q in range(9):
            b, e = q // 3, q % 3
            x9[m, :, C * q : C * (q + 1)] = sx[m, e, cols * b : cols * b + mp, :].astype(bf)

    for k in range(27):
        load_one(k).wait()

    conv[...] = jnp.dot(
        x9[...].reshape(tmn * mp, 9 * C), r1[...], preferred_element_type=f32
    )
    for t in range(tmn):
        hidden = conv[t * mp : t * mp + cells, 2 * C :]
        for a in range(2):
            s = t - 2 + a
            if s >= 0:
                hidden = hidden + conv[s * mp : s * mp + cells, C * a : C * (a + 1)]
        squash = jax.nn.sigmoid(hidden)
        gate[t] = squash * (1.0 + hidden * (1.0 - squash))
        at[(t + 2) * cwp : (t + 3) * cwp, :cells] = tall((hidden * squash).astype(bf))
    for s in range(tmn):
        for q in range(9):
            xt[s, cwp * q : cwp * (q + 1), :mp] = tall(x9[s, :, C * q : C * (q + 1)])

    for m in range(tmn):

        @pl.when(tm != m)
        def _():
            arrived(gat.at[1, m], blk_recv.at[1, m])

        spread(sc.at[m], gat[1, m].astype(f32), hal[m, 1].astype(f32))
        for q in range(9):
            b, e = q // 3, q % 3
            c9[m, :mp, C * q : C * (q + 1)] = sc[m, 2 - e, cols * (2 - b) : cols * (2 - b) + mp, :].astype(bf)

    def send_pair(tensor, r):
        return remote(
            pstage.at[tensor, r],
            pland.at[tensor, row],
            pair_send.at[tensor, r],
            pair_recv.at[tensor, row],
            (tm, r, col),
        )

    def send_pairs(tensor):
        for r in range(rn):

            @pl.when(row != r)
            def _():
                send_pair(tensor, r).start()

    def send_piece(tensor, z):
        return remote(
            stage.at[tensor, z], landed.at[tensor, col], rs_send.at[tensor, z], rs_recv.at[tensor, col], (tm, row, z)
        )

    group = slots * chunk_pad // zn

    def scatter(tensor):
        pp[:taps, :] = part[tensor, row]
        for r in range(rn):

            @pl.when(row != r)
            def _():
                arrived(pland.at[tensor, r], pair_recv.at[tensor, r])
                pp[:taps, :] += pland[tensor, r].astype(f32)

        for z in range(zn):
            stage[tensor, z] = jnp.concatenate(
                [pp[group * q : group * (q + 1), ochunk * z : ochunk * (z + 1)] for q in range(zn)],
                axis=1,
            ).astype(bf)
        for z in range(zn):

            @pl.when(col != z)
            def _():
                send_piece(tensor, z).start()

    total = None
    for s in range(tmn):
        got = jnp.dot(at[s * cwp : (s + 3) * cwp, :], c9[s], preferred_element_type=f32)
        total = got if total is None else total + got
    for a in range(3):
        for r in range(rn):
            for q in range(9):
                k = 9 * a + q
                piece = total[a * cwp + r * chunk_pad : a * cwp + (r + 1) * chunk_pad, C * q : C * (q + 1)]
                part[1, r, k * chunk_pad : (k + 1) * chunk_pad, :] = piece
                pstage[1, r, k * chunk_pad : (k + 1) * chunk_pad, :] = piece.astype(bf)
    send_pairs(1)

    for k in range(27):
        load_two(k).wait()
    conv[...] = lax.dot_general(
        c9[:, :mp, :].reshape(tmn * mp, 9 * C), r2[...], NT, preferred_element_type=f32
    )
    for t in range(tmn):
        grad = conv[t * mp : t * mp + cells, 2 * C :]
        for a in range(2):
            s = t + 2 - a
            if s < tmn:
                grad = grad + conv[s * mp : s * mp + cells, C * a : C * (a + 1)]
        grad = (grad * gate[t]).astype(bf)
        ghb[t, :cells, :] = grad
        ghf[t * cells : (t + 1) * cells, :] = grad.astype(f32)

    own3[...] = ghf[pl.ds(pl.multiple_of(tm * cells, 8), 3 * cells), :]
    for h in range(2):
        gedge[h] = own3[pl.ds(h * (cols - 1), 3 * rows, stride=cols), :].astype(bf)
    for v in range(2):
        grim[v] = jnp.concatenate(
            [
                own3[j * cells + v * (cells - cols) : j * cells + v * (cells - cols) + cols, :]
                for j in range(3)
            ],
            axis=0,
        ).astype(bf)
    grims = near(grim, gedge, grim_in, gedge_in, gcorner_in, gnear_sem)
    start_all(grims)

    scatter(1)

    total = None
    for s in range(tmn):
        right_side = jnp.concatenate([ghb[s + 2], ghb[s + 1], ghb[s]], axis=1)
        got = jnp.dot(xt[s], right_side, preferred_element_type=f32)
        total = got if total is None else total + got
    for q in range(9):
        for r in range(rn):
            for a in range(3):
                k = 9 * a + q
                piece = total[q * cwp + r * chunk_pad : q * cwp + (r + 1) * chunk_pad, C * a : C * (a + 1)]
                part[0, r, k * chunk_pad : (k + 1) * chunk_pad, :] = piece
                pstage[0, r, k * chunk_pad : (k + 1) * chunk_pad, :] = piece.astype(bf)
    send_pairs(0)

    await_all(grims)
    assemble(gf, 3, grim_in, gedge_in, gcorner_in)
    for j in range(3):
        spread(sh.at[j], own3[j * cells : (j + 1) * cells, :], gf[j])
        for q in range(9):
            b, e = q // 3, q % 3
            lane = C * (3 * q + 2 - j)
            imc[:, lane : lane + C] = sh[j, 2 - e, cols * (2 - b) : cols * (2 - b) + mp, :].astype(bf)

    scatter(0)

    total = None
    for q in range(9):
        got = lax.dot_general(
            imc[:, 3 * C * q : 3 * C * (q + 1)], r1[C * q : C * (q + 1), :], NT, preferred_element_type=f32
        )
        total = got if total is None else total + got
    back_ref[...] = flat[1] + total[:cells]

    for tensor in (1, 0):
        acc[tensor] = stage[tensor, col].astype(f32)
        for z in range(zn):

            @pl.when(col != z)
            def _():
                arrived(landed.at[tensor, z], rs_recv.at[tensor, z])
                acc[tensor] += landed[tensor, z].astype(f32)

    for which in range(2):
        for d in range(1, tmn):
            send_block(which, d).wait_send()
        for r in range(rn):

            @pl.when(row != r)
            def _():
                send_pair(which, r).wait_send()

        for z in range(zn):

            @pl.when(col != z)
            def _():
                send_piece(which, z).wait_send()

    for d in range(1, tmn):
        send_halo(d).wait_send()
    drain_all(rims)
    drain_all(grims)


def finish(zn, chunk, chunk_pad, slots, back_ref, acc_ref, out_ref, one_ref, two_ref):
    ochunk = C // zn
    out_ref[...] = back_ref[...]
    for tensor, out in enumerate((one_ref, two_ref)):
        got = acc_ref[tensor]
        whole = jnp.concatenate(
            [got[:, ochunk * q : ochunk * (q + 1)] for q in range(zn)], axis=0
        ).reshape(slots, chunk_pad, ochunk)
        out[...] = whole[:27, :chunk, :]


def body(sizes, inputs, cotangent, weight_one, weight_two):
    tmn, rn, zn = sizes
    _, rows, cols, channels = inputs.shape
    cells = rows * cols
    chunk = channels // (tmn * rn)
    chunk_pad = max(16, chunk)
    slots = 28
    lift = (rows + 2) * cols
    mp = -(-cells // 16) * 16
    kp = -(-cells // 128) * 128
    hs = -(-(2 * cols + 2 * (-(-(rows + 2) // 8) * 8)) // 16) * 16
    cwp = rn * chunk_pad
    taps = 27 * chunk_pad
    dims = (tmn, rn, zn, rows, cols, chunk, chunk_pad, slots)
    vmem = pl.BlockSpec(memory_space=pltpu.VMEM)
    bf, f32 = jnp.bfloat16, jnp.float32
    group = slots * chunk_pad // zn
    dma = pltpu.SemaphoreType.DMA
    lifted = lift + mp - cells
    back, acc = pl.pallas_call(
        functools.partial(kernel, dims),
        out_shape=(
            jax.ShapeDtypeStruct((cells, channels), f32),
            jax.ShapeDtypeStruct((2, group, channels), f32),
        ),
        in_specs=[pl.BlockSpec(memory_space=pl.ANY)] * 4,
        out_specs=(vmem,) * 2,
        scratch_shapes=[
            pltpu.VMEM((2, tmn, cells, channels), bf),
            pltpu.VMEM((2, cells, channels), f32),
            pltpu.VMEM((2, hs, channels), f32),
            pltpu.VMEM((tmn, 2, hs, channels), bf),
            pltpu.VMEM((tmn, 3, lifted, channels), f32),
            pltpu.VMEM((tmn, 3, lifted, channels), f32),
            pltpu.VMEM((tmn, mp, 9 * channels), bf),
            pltpu.VMEM((tmn, kp, 9 * channels), bf),
            pltpu.VMEM((9 * channels, 3 * channels), bf),
            pltpu.VMEM((3 * channels, 9 * channels), bf),
            pltpu.VMEM((tmn * mp, 3 * channels), f32),
            pltpu.VMEM((tmn, cells, channels), f32),
            pltpu.VMEM(((tmn + 2) * cwp, kp), bf),
            pltpu.VMEM((tmn, 9 * cwp, kp), bf),
            pltpu.VMEM((tmn + 2, kp, channels), bf),
            pltpu.VMEM(((tmn + 2) * cells, channels), f32),
            pltpu.VMEM((3 * cells, channels), f32),
            pltpu.VMEM((3, hs, channels), f32),
            pltpu.VMEM((3, 3, lifted, channels), f32),
            pltpu.VMEM((mp, 27 * channels), bf),
            pltpu.VMEM((2, rn, taps, channels), f32),
            pltpu.VMEM((2, rn, taps, channels), bf),
            pltpu.VMEM((2, rn, taps, channels), bf),
            pltpu.VMEM((slots * chunk_pad, channels), f32),
            pltpu.VMEM((2, zn, group, channels), bf),
            pltpu.VMEM((2, zn, group, channels), bf),
            pltpu.VMEM((2, 2 * cols, channels), bf),
            pltpu.VMEM((2, 2 * rows, channels), bf),
            pltpu.VMEM((2, 2 * cols, channels), bf),
            pltpu.VMEM((2, 2 * rows, channels), bf),
            pltpu.VMEM((2, 2, 2 * rows, channels), bf),
            pltpu.VMEM((2, 3 * cols, channels), bf),
            pltpu.VMEM((2, 3 * rows, channels), bf),
            pltpu.VMEM((2, 3 * cols, channels), bf),
            pltpu.VMEM((2, 3 * rows, channels), bf),
            pltpu.VMEM((2, 2, 3 * rows, channels), bf),
            dma((2,)),
            dma((27,)),
            dma((27,)),
            dma((2, tmn)),
            dma((2, tmn)),
            dma((tmn,)),
            dma((tmn,)),
            dma((2, 8)),
            dma((2, 8)),
            dma((2, rn)),
            dma((2, rn)),
            dma((2, zn)),
            dma((2, zn)),
        ],
        compiler_params=pltpu.CompilerParams(
            collective_id=0, has_side_effects=True, vmem_limit_bytes=60 * 1024 * 1024
        ),
    )(
        inputs.reshape(cells, channels),
        cotangent.reshape(cells, channels),
        weight_one.reshape(27 * channels, channels),
        weight_two.reshape(27 * channels, channels),
    )
    back, one, two = pl.pallas_call(
        functools.partial(finish, zn, chunk, chunk_pad, slots),
        out_shape=(
            jax.ShapeDtypeStruct((cells, channels), f32),
            jax.ShapeDtypeStruct((27, chunk, channels // zn), f32),
            jax.ShapeDtypeStruct((27, chunk, channels // zn), f32),
        ),
        in_specs=[vmem] * 2,
        out_specs=(vmem,) * 3,
    )(back, acc)
    return back.reshape(1, rows, cols, channels), one, two


def solution(mesh):
    sizes = (mesh.shape["tm"], mesh.shape["rows"], mesh.shape["cols"])
    placed = (P("tm", "rows", "cols", None), P("tm", "rows", "cols", None), P(), P())
    return jax.shard_map(
        functools.partial(body, sizes),
        mesh=mesh,
        in_specs=placed,
        out_specs=(
            P("tm", "rows", "cols", None),
            P(None, ("tm", "rows"), "cols"),
            P(None, ("tm", "rows"), "cols"),
        ),
        check_vma=False,
    )
```

time: 29.5 us -> 28.4 us (0.963)
  Pallas kernels: 28.7 us -> 27.5 us
    pallas_call x1, Pallas kernels: 26.9 us -> 25.7 us  [body(): pl.pallas_call(functools.partial(kernel, dims), out_shape=(jax.ShapeDtype...]
where the time goes in v1:
time: 28.4 us; the launch traced here: 28.2 us
  Pallas kernels  27.5 us (97%)
  between operations  0.64 us (2%)
    pallas_call x1, Pallas kernels, body(): pl.pallas_call(functools.partial(kernel, dims), out_shape=(jax.ShapeDtype...  25.7 us
    pallas_call x1, Pallas kernels, body(): pl.pallas_call(functools.partial(finish, zn, chunk, chunk_pad, slots), ou...  1.8 us

profile of v1, /device:TPU:0, one launch (start us, length us, event | category | flops | bytes accessed | tf_op | source)
XLA Modules:
  0.0 28.2 jit_solution(14026276727928308666)
XLA Ops:
  0.6 25.7 %shard_map.67 = (f32[136,128]{1,0:T(8,128)}, f32[2,112,128]{2,1,0:T(8,128)}) custom-call(bf16[136,128]{1,0:T(8,128)(2,1)} %bitcast.7, bf16[136,128]{1,0:T(8,128)(2,1)} %bitcast.8, bf16[3456,128]{1,0:T(8,128)(2,1)} %bitcast.5, bf16[3456,128]{1,0:T(8,128)(2,1)} %bitcast.6), custom_call_target="tpu_custom_call" | custom-call | tf_op jit(solution)/shard_map/pallas_call | solution.py:538
  26.4 1.8 %shard_map.68 = (f32[136,128]{1,0:T(8,128)}, f32[27,16,32]{2,1,0:T(8,128)}, f32[27,16,32]{2,1,0:T(8,128)}) custom-call(f32[136,128]{1,0:T(8,128)} %get-tuple-element.8.back_ref, f32[2,112,128]{2,1,0:T(8,128)} %get-tuple-element.9.acc_ref), custom_call_target="tpu_custom_call" | custom-call | tf_op jit(solution)/shard_map/pallas_call | solution.py:606

commit v2 on v1

--- a/solution.py
+++ b/solution.py
@@ -22,8 +22,6 @@
     acc,
     gat,
     flat,
-    hf,
-    hal,
     sx,
     sc,
     x9,
@@ -48,9 +46,10 @@
     landed,
     rim,
     edge,
+    tip,
     rim_in,
     edge_in,
-    corner_in,
+    tip_in,
     grim,
     gedge,
     grim_in,
@@ -61,9 +60,8 @@
     w2_sem,
     blk_send,
     blk_recv,
-    hal_send,
-    hal_recv,
-    near_sem,
+    near_send,
+    near_recv,
     gnear_sem,
     pair_send,
     pair_recv,
@@ -85,28 +83,59 @@
     side = (col > 0, col < zn - 1)
     step = (-1, 1)
 
+    def partner(d):
+        if tmn == 4:
+            flips = (tm, tm + 1 - 2 * lax.rem(tm, 2), tm + 2 - 4 * (tm // 2), 3 - tm)
+            return flips[d]
+        return lax.rem(tm + d, tmn)
+
+    blocks = (x_ref, c_ref)
+
+    def keep(which):
+        return pltpu.make_async_copy(blocks[which], gat.at[which, tm], own_sem.at[which])
+
+    keep(0).start()
+    keep(1).start()
     barrier = pltpu.get_barrier_semaphore()
 
     def greet(place):
         pl.semaphore_signal(barrier, inc=1, device_id=place, device_id_type=MESH)
 
-    for d in range(1, tmn):
-        greet((lax.rem(tm + d, tmn), row, col))
-    for d in range(1, rn):
-        greet((tm, lax.rem(row + d, rn), col))
-    for d in range(1, zn):
-        greet((tm, row, lax.rem(col + d, zn)))
+    for z in range(zn):
+
+        @pl.when(jnp.logical_or(col - z > 1, z - col > 1))
+        def _():
+            greet((tm, row, z))
+
+    for d in range(tmn - 1, 0, -1):
+        greet((partner(d), row, col))
     for v in range(2):
         for h in range(2):
 
             @pl.when(jnp.logical_and(vert[v], side[h]))
             def _():
-                greet((tm, row + step[v], col + step[h]))
-
-    blocks = (x_ref, c_ref)
-
-    def keep(which):
-        return pltpu.make_async_copy(blocks[which], gat.at[which, tm], own_sem.at[which])
+                for d in range(tmn - 1, -1, -1):
+                    greet((partner(d), row + step[v], col + step[h]))
+
+    for h in range(2):
+
+        @pl.when(side[h])
+        def _():
+            for d in range(tmn - 1, -1, -1):
+                greet((partner(d), row, col + step[h]))
+
+    for v in range(2):
+
+        @pl.when(vert[v])
+        def _():
+            for d in range(tmn - 1, -1, -1):
+                greet((partner(d), row + step[v], col))
+
+    for r in range(rn if rn > 2 else 0):
+
+        @pl.when(jnp.logical_or(row - r > 1, r - row > 1))
+        def _():
+            greet((tm, r, col))
 
     def load_one(k):
         a, q = k // 9, k % 9
@@ -120,26 +149,35 @@
             w2_ref.at[pl.ds(C * k, C), :], r2.at[pl.ds(C * a, C), pl.ds(C * q, C)], w2_sem.at[k]
         )
 
-    keep(0).start()
-    keep(1).start()
     for k in range(27):
         load_one(k).start()
     for k in range(27):
         load_two(k).start()
 
-    hf[...] = jnp.zeros(hf.shape, f32)
+    for v in range(2):
+
+        @pl.when(jnp.logical_not(vert[v]))
+        def _():
+            rim_in[:, :, v] = jnp.zeros((2, tmn, cols, C), bf)
+            tip_in[:, :, v] = jnp.zeros((2, tmn, 2, 8, C), bf)
+
+    for h in range(2):
+
+        @pl.when(jnp.logical_not(side[h]))
+        def _():
+            edge_in[:, :, h] = jnp.zeros((2, tmn, rows, C), bf)
+            tip_in[:, :, :, h] = jnp.zeros((2, tmn, 2, 8, C), bf)
 
     for which in range(2):
         keep(which).wait()
         flat[which] = gat[which, tm].astype(f32)
         for h in range(2):
-            edge[h, which * rows : (which + 1) * rows, :] = flat[
-                which, pl.ds(h * (cols - 1), rows, stride=cols), :
-            ].astype(bf)
+            edge[which, h] = flat[which, pl.ds(h * (cols - 1), rows, stride=cols), :].astype(bf)
         for v in range(2):
-            rim[v, which * cols : (which + 1) * cols, :] = flat[
-                which, v * (cells - cols) : v * (cells - cols) + cols, :
-            ].astype(bf)
+            line = flat[which, v * (cells - cols) : v * (cells - cols) + cols, :]
+            rim[which, v] = line.astype(bf)
+            for h in range(2):
+                tip[which, v, h] = jnp.broadcast_to(line[h * (cols - 1) : h * (cols - 1) + 1], (8, C)).astype(bf)
 
     def remote(src, dst, send, recv, place):
         return pltpu.make_async_remote_copy(
@@ -233,27 +271,26 @@
                         take = q * rows + (1 - v) * (rows - 1)
                         dst[q, put : put + 1, :] = got[take : take + 1]
 
-    def spread(dst, v, h):
-        top, bottom = h[:cols], h[cols : 2 * cols]
+    def spread(dst, v, top, bottom, sides, tips):
         dst[1, :cols, :] = top
         dst[1, cols : cols + cells, :] = v
         dst[1, cols + cells : lift, :] = bottom
         dst[0, 1 : cols + 1, :] = top
         dst[0, cols + 1 : cols + cells + 1, :] = v
         dst[0, cols + cells + 1 : lift, :] = bottom[: cols - 1]
-        dst[0, pl.ds(0, rows + 2, stride=cols), :] = h[left : left + rows + 2]
+        dst[0, :1, :] = tips[0][0]
+        dst[0, pl.ds(cols, rows, stride=cols), :] = sides[0]
+        dst[0, cols + cells : cols + cells + 1, :] = tips[1][0]
         dst[2, : cols - 1, :] = top[1:]
         dst[2, cols - 1 : cols + cells - 1, :] = v
         dst[2, cols + cells - 1 : lift - 1, :] = bottom
-        dst[2, pl.ds(cols - 1, rows + 2, stride=cols), :] = h[right : right + rows + 2]
-
-    corners = (vert[0].astype(jnp.int32) + vert[1].astype(jnp.int32)) * (
-        side[0].astype(jnp.int32) + side[1].astype(jnp.int32)
-    )
-    pl.semaphore_wait(barrier, tmn + rn + zn - 3 + corners)
-
-    rims = near(rim, edge, rim_in, edge_in, corner_in, near_sem)
-    start_all(rims)
+        dst[2, cols - 1 : cols, :] = tips[0][1]
+        dst[2, pl.ds(2 * cols - 1, rows, stride=cols), :] = sides[1]
+        dst[2, lift - 1 : lift, :] = tips[1][1]
+
+    nv = vert[0].astype(jnp.int32) + vert[1].astype(jnp.int32)
+    nh = side[0].astype(jnp.int32) + side[1].astype(jnp.int32)
+    pl.semaphore_wait(barrier, tmn * (1 + nv) * (1 + nh) - 1 + zn - 1 - nh + rn - 1 - nv)
 
     def send_block(which, d):
         return remote(
@@ -261,16 +298,101 @@
             gat.at[which, tm],
             blk_send.at[which, d],
             blk_recv.at[which, tm],
-            (lax.rem(tm + d, tmn), row, col),
-        )
-
-    def send_halo(d):
+            (partner(d), row, col),
+        )
+
+    def send_rim(which, v, d):
         return remote(
-            hal.at[tm], hal.at[tm], hal_send.at[d], hal_recv.at[tm], (lax.rem(tm + d, tmn), row, col)
-        )
-
-    for d in range(1, tmn):
-        send_block(0, d).start()
+            rim.at[which, v],
+            rim_in.at[which, tm, 1 - v],
+            near_send.at[which, v, d],
+            near_recv.at[which, 1 - v, tm],
+            (partner(d), row + step[v], col),
+        )
+
+    def send_edge(which, h, d):
+        return remote(
+            edge.at[which, h],
+            edge_in.at[which, tm, 1 - h],
+            near_send.at[which, 2 + h, d],
+            near_recv.at[which, 3 - h, tm],
+            (partner(d), row, col + step[h]),
+        )
+
+    def send_tip(which, v, h, d):
+        return remote(
+            tip.at[which, v, h],
+            tip_in.at[which, tm, 1 - v, 1 - h],
+            near_send.at[which, 4 + 2 * v + h, d],
+            near_recv.at[which, 4 + 2 * (1 - v) + 1 - h, tm],
+            (partner(d), row + step[v], col + step[h]),
+        )
+
+    def each_near(which, act):
+        for h in range(2):
+
+            @pl.when(side[h])
+            def _():
+                for d in range(tmn - 1, -1, -1):
+                    act(send_edge(which, h, d))
+
+        for v in range(2):
+
+            @pl.when(vert[v])
+            def _():
+                for d in range(tmn - 1, -1, -1):
+                    act(send_rim(which, v, d))
+
+        for v in range(2):
+            for h in range(2):
+
+                @pl.when(jnp.logical_and(vert[v], side[h]))
+                def _():
+                    for d in range(tmn - 1, -1, -1):
+                        act(send_tip(which, v, h, d))
+
+    for which in range(2):
+        each_near(which, lambda copy: copy.start())
+        for d in range(tmn - 1, 0, -1):
+            send_block(which, d).start()
+
+    def receive(which, ds, dst):
+        for d in ds[ds[0] == 0 :]:
+            arrived(gat.at[which, partner(d)], blk_recv.at[which, partner(d)])
+        for h in range(2):
+
+            @pl.when(side[h])
+            def _():
+                for d in ds:
+                    arrived(edge_in.at[which, partner(d), h], near_recv.at[which, 2 + h, partner(d)])
+
+        for v in range(2):
+
+            @pl.when(vert[v])
+            def _():
+                for d in ds:
+                    arrived(rim_in.at[which, partner(d), v], near_recv.at[which, v, partner(d)])
+
+        for v in range(2):
+            for h in range(2):
+
+                @pl.when(jnp.logical_and(vert[v], side[h]))
+                def _():
+                    for d in ds:
+                        arrived(tip_in.at[which, partner(d), v, h], near_recv.at[which, 4 + 2 * v + h, partner(d)])
+
+        for d in ds:
+            s = partner(d)
+            spread(
+                dst.at[d],
+                gat[which, s].astype(f32),
+                rim_in[which, s, 0].astype(f32),
+                rim_in[which, s, 1].astype(f32),
+                [edge_in[which, s, h].astype(f32) for h in range(2)],
+                [[tip_in[which, s, v, h].astype(f32)[:1] for h in range(2)] for v in range(2)],
+            )
+
+    groups = [list(range(d, min(d + 2, tmn))) for d in range(0, tmn, 2)]
 
     for tail in (sx, sc):
         for s in range(tmn):
@@ -304,56 +426,39 @@
     def tall(src):
         return lax.dot_general(picked, src, NT, preferred_element_type=f32).astype(bf)
 
-    await_all(rims)
-    assemble(hf, 2, rim_in, edge_in, corner_in)
-    for which in range(2):
-        hal[tm, which] = hf[which].astype(bf)
-    for d in range(1, tmn):
-        send_halo(d).start()
-    for d in range(1, tmn):
-        send_block(1, d).start()
-
-    for m in range(tmn):
-
-        @pl.when(tm != m)
-        def _():
-            arrived(gat.at[0, m], blk_recv.at[0, m])
-            arrived(hal.at[m], hal_recv.at[m])
-
-        spread(sx.at[m], gat[0, m].astype(f32), hal[m, 0].astype(f32))
-        for q in range(9):
-            b, e = q // 3, q % 3
-            x9[m, :, C * q : C * (q + 1)] = sx[m, e, cols * b : cols * b + mp, :].astype(bf)
-
-    for k in range(27):
-        load_one(k).wait()
-
-    conv[...] = jnp.dot(
-        x9[...].reshape(tmn * mp, 9 * C), r1[...], preferred_element_type=f32
-    )
+    def choose_x(ds):
+        for d in ds:
+            for q in range(9):
+                xt[d, cwp * q : cwp * (q + 1), :mp] = tall(x9[d, :, C * q : C * (q + 1)])
+
+    for ds in groups:
+        receive(0, ds, sx)
+        for d in ds:
+            for q in range(9):
+                b, e = q // 3, q % 3
+                x9[d, :, C * q : C * (q + 1)] = sx[d, e, cols * b : cols * b + mp, :].astype(bf)
+        if ds[0] == 0:
+            for k in range(27):
+                load_one(k).wait()
+        got = jnp.dot(
+            x9[ds[0] : ds[-1] + 1].reshape(len(ds) * mp, 9 * C), r1[...], preferred_element_type=f32
+        )
+        for d in ds:
+            conv[partner(d)] = got[(d - ds[0]) * mp : (d - ds[0] + 1) * mp]
+        if ds is not groups[-1]:
+            choose_x(ds)
     for t in range(tmn):
-        hidden = conv[t * mp : t * mp + cells, 2 * C :]
+        hidden = conv[t, :cells, 2 * C :]
         for a in range(2):
             s = t - 2 + a
             if s >= 0:
-                hidden = hidden + conv[s * mp : s * mp + cells, C * a : C * (a + 1)]
+                hidden = hidden + conv[s, :cells, C * a : C * (a + 1)]
         squash = jax.nn.sigmoid(hidden)
         gate[t] = squash * (1.0 + hidden * (1.0 - squash))
         at[(t + 2) * cwp : (t + 3) * cwp, :cells] = tall((hidden * squash).astype(bf))
-    for s in range(tmn):
-        for q in range(9):
-            xt[s, cwp * q : cwp * (q + 1), :mp] = tall(x9[s, :, C * q : C * (q + 1)])
-
-    for m in range(tmn):
-
-        @pl.when(tm != m)
-        def _():
-            arrived(gat.at[1, m], blk_recv.at[1, m])
-
-        spread(sc.at[m], gat[1, m].astype(f32), hal[m, 1].astype(f32))
-        for q in range(9):
-            b, e = q // 3, q % 3
-            c9[m, :mp, C * q : C * (q + 1)] = sc[m, 2 - e, cols * (2 - b) : cols * (2 - b) + mp, :].astype(bf)
+    choose_x(groups[-1])
+    for k in range(27):
+        load_two(k).wait()
 
     def send_pair(tensor, r):
         return remote(
@@ -399,29 +504,36 @@
                 send_piece(tensor, z).start()
 
     total = None
-    for s in range(tmn):
-        got = jnp.dot(at[s * cwp : (s + 3) * cwp, :], c9[s], preferred_element_type=f32)
-        total = got if total is None else total + got
-    for a in range(3):
-        for r in range(rn):
+    for ds in groups:
+        receive(1, ds, sc)
+        for d in ds:
             for q in range(9):
-                k = 9 * a + q
-                piece = total[a * cwp + r * chunk_pad : a * cwp + (r + 1) * chunk_pad, C * q : C * (q + 1)]
-                part[1, r, k * chunk_pad : (k + 1) * chunk_pad, :] = piece
-                pstage[1, r, k * chunk_pad : (k + 1) * chunk_pad, :] = piece.astype(bf)
-    send_pairs(1)
-
-    for k in range(27):
-        load_two(k).wait()
-    conv[...] = lax.dot_general(
-        c9[:, :mp, :].reshape(tmn * mp, 9 * C), r2[...], NT, preferred_element_type=f32
-    )
+                b, e = q // 3, q % 3
+                c9[d, :mp, C * q : C * (q + 1)] = sc[d, 2 - e, cols * (2 - b) : cols * (2 - b) + mp, :].astype(bf)
+        for d in ds:
+            lines = pl.ds(pl.multiple_of(partner(d) * cwp, 16), 3 * cwp)
+            got = jnp.dot(at[lines, :], c9[d], preferred_element_type=f32)
+            total = got if total is None else total + got
+        if ds is groups[-1]:
+            for a in range(3):
+                for r in range(rn):
+                    for q in range(9):
+                        k = 9 * a + q
+                        piece = total[a * cwp + r * chunk_pad : a * cwp + (r + 1) * chunk_pad, C * q : C * (q + 1)]
+                        part[1, r, k * chunk_pad : (k + 1) * chunk_pad, :] = piece
+                        pstage[1, r, k * chunk_pad : (k + 1) * chunk_pad, :] = piece.astype(bf)
+            send_pairs(1)
+        got = lax.dot_general(
+            c9[ds[0] : ds[-1] + 1, :mp, :].reshape(len(ds) * mp, 9 * C), r2[...], NT, preferred_element_type=f32
+        )
+        for d in ds:
+            conv[partner(d)] = got[(d - ds[0]) * mp : (d - ds[0] + 1) * mp]
     for t in range(tmn):
-        grad = conv[t * mp : t * mp + cells, 2 * C :]
+        grad = conv[t, :cells, 2 * C :]
         for a in range(2):
             s = t + 2 - a
             if s < tmn:
-                grad = grad + conv[s * mp : s * mp + cells, C * a : C * (a + 1)]
+                grad = grad + conv[s, :cells, C * a : C * (a + 1)]
         grad = (grad * gate[t]).astype(bf)
         ghb[t, :cells, :] = grad
         ghf[t * cells : (t + 1) * cells, :] = grad.astype(f32)
@@ -443,9 +555,10 @@
     scatter(1)
 
     total = None
-    for s in range(tmn):
+    for d in range(tmn):
+        s = partner(d)
         right_side = jnp.concatenate([ghb[s + 2], ghb[s + 1], ghb[s]], axis=1)
-        got = jnp.dot(xt[s], right_side, preferred_element_type=f32)
+        got = jnp.dot(xt[d], right_side, preferred_element_type=f32)
         total = got if total is None else total + got
     for q in range(9):
         for r in range(rn):
@@ -456,17 +569,24 @@
                 pstage[0, r, k * chunk_pad : (k + 1) * chunk_pad, :] = piece.astype(bf)
     send_pairs(0)
 
+    scatter(0)
+
     await_all(grims)
     assemble(gf, 3, grim_in, gedge_in, gcorner_in)
     for j in range(3):
-        spread(sh.at[j], own3[j * cells : (j + 1) * cells, :], gf[j])
+        spread(
+            sh.at[j],
+            own3[j * cells : (j + 1) * cells, :],
+            gf[j, :cols, :],
+            gf[j, cols : 2 * cols, :],
+            [gf[j, base + 1 : base + 1 + rows, :] for base in (left, right)],
+            [[gf[j, base + put : base + put + 1, :] for base in (left, right)] for put in (0, rows + 1)],
+        )
         for q in range(9):
             b, e = q // 3, q % 3
             lane = C * (3 * q + 2 - j)
             imc[:, lane : lane + C] = sh[j, 2 - e, cols * (2 - b) : cols * (2 - b) + mp, :].astype(bf)
 
-    scatter(0)
-
     total = None
     for q in range(9):
         got = lax.dot_general(
@@ -499,9 +619,8 @@
             def _():
                 send_piece(which, z).wait_send()
 
-    for d in range(1, tmn):
-        send_halo(d).wait_send()
-    drain_all(rims)
+    for which in range(2):
+        each_near(which, lambda copy: copy.wait_send())
     drain_all(grims)
 
 
@@ -546,15 +665,13 @@
         scratch_shapes=[
             pltpu.VMEM((2, tmn, cells, channels), bf),
             pltpu.VMEM((2, cells, channels), f32),
-            pltpu.VMEM((2, hs, channels), f32),
-            pltpu.VMEM((tmn, 2, hs, channels), bf),
             pltpu.VMEM((tmn, 3, lifted, channels), f32),
             pltpu.VMEM((tmn, 3, lifted, channels), f32),
             pltpu.VMEM((tmn, mp, 9 * channels), bf),
             pltpu.VMEM((tmn, kp, 9 * channels), bf),
             pltpu.VMEM((9 * channels, 3 * channels), bf),
             pltpu.VMEM((3 * channels, 9 * channels), bf),
-            pltpu.VMEM((tmn * mp, 3 * channels), f32),
+            pltpu.VMEM((tmn, mp, 3 * channels), f32),
             pltpu.VMEM((tmn, cells, channels), f32),
             pltpu.VMEM(((tmn + 2) * cwp, kp), bf),
             pltpu.VMEM((tmn, 9 * cwp, kp), bf),
@@ -570,11 +687,12 @@
             pltpu.VMEM((slots * chunk_pad, channels), f32),
             pltpu.VMEM((2, zn, group, channels), bf),
             pltpu.VMEM((2, zn, group, channels), bf),
-            pltpu.VMEM((2, 2 * cols, channels), bf),
-            pltpu.VMEM((2, 2 * rows, channels), bf),
-            pltpu.VMEM((2, 2 * cols, channels), bf),
-            pltpu.VMEM((2, 2 * rows, channels), bf),
-            pltpu.VMEM((2, 2, 2 * rows, channels), bf),
+            pltpu.VMEM((2, 2, cols, channels), bf),
+            pltpu.VMEM((2, 2, rows, channels), bf),
+            pltpu.VMEM((2, 2, 2, 8, channels), bf),
+            pltpu.VMEM((2, tmn, 2, cols, channels), bf),
+            pltpu.VMEM((2, tmn, 2, rows, channels), bf),
+            pltpu.VMEM((2, tmn, 2, 2, 8, channels), bf),
             pltpu.VMEM((2, 3 * cols, channels), bf),
             pltpu.VMEM((2, 3 * rows, channels), bf),
             pltpu.VMEM((2, 3 * cols, channels), bf),
@@ -585,9 +703,8 @@
             dma((27,)),
             dma((2, tmn)),
             dma((2, tmn)),
-            dma((tmn,)),
-            dma((tmn,)),
-            dma((2, 8)),
+            dma((2, 8, tmn)),
+            dma((2, 8, tmn)),
             dma((2, 8)),
             dma((2, rn)),
             dma((2, rn)),

time: 28.4 us -> 28.5 us (level)
  no operation moved by 1% of the time
where the time goes in v2:
time: 28.5 us; the launch traced here: 28.3 us
  Pallas kernels  27.6 us (97%)
  between operations  0.64 us (2%)
    pallas_call x1, Pallas kernels, body(): pl.pallas_call(functools.partial(kernel, dims), out_shape=(jax.ShapeDtype...  25.8 us
    pallas_call x1, Pallas kernels, body(): pl.pallas_call(functools.partial(finish, zn, chunk, chunk_pad, slots), ou...  1.8 us

profile of v2, /device:TPU:0, one launch (start us, length us, event | category | flops | bytes accessed | tf_op | source)
XLA Modules:
  0.0 28.3 jit_solution(17898380092291133952)
XLA Ops:
  0.6 25.8 %shard_map.67 = (f32[136,128]{1,0:T(8,128)}, f32[2,112,128]{2,1,0:T(8,128)}) custom-call(bf16[136,128]{1,0:T(8,128)(2,1)} %bitcast.7, bf16[136,128]{1,0:T(8,128)(2,1)} %bitcast.8, bf16[3456,128]{1,0:T(8,128)(2,1)} %bitcast.5, bf16[3456,128]{1,0:T(8,128)(2,1)} %bitcast.6), custom_call_target="tpu_custom_call" | custom-call | tf_op jit(solution)/shard_map/pallas_call | solution.py:657
  26.5 1.8 %shard_map.68 = (f32[136,128]{1,0:T(8,128)}, f32[27,16,32]{2,1,0:T(8,128)}, f32[27,16,32]{2,1,0:T(8,128)}) custom-call(f32[136,128]{1,0:T(8,128)} %get-tuple-element.8.back_ref, f32[2,112,128]{2,1,0:T(8,128)} %get-tuple-element.9.acc_ref), custom_call_target="tpu_custom_call" | custom-call | tf_op jit(solution)/shard_map/pallas_call | solution.py:723

commit v3 on v2

--- a/solution.py
+++ b/solution.py
@@ -19,7 +19,8 @@
     w1_ref,
     w2_ref,
     back_ref,
-    acc,
+    one_ref,
+    two_ref,
     gat,
     flat,
     sx,
@@ -328,19 +329,19 @@
             (partner(d), row + step[v], col + step[h]),
         )
 
-    def each_near(which, act):
+    def each_near(which, ds, act):
         for h in range(2):
 
             @pl.when(side[h])
             def _():
-                for d in range(tmn - 1, -1, -1):
+                for d in ds:
                     act(send_edge(which, h, d))
 
         for v in range(2):
 
             @pl.when(vert[v])
             def _():
-                for d in range(tmn - 1, -1, -1):
+                for d in ds:
                     act(send_rim(which, v, d))
 
         for v in range(2):
@@ -348,13 +349,16 @@
 
                 @pl.when(jnp.logical_and(vert[v], side[h]))
                 def _():
-                    for d in range(tmn - 1, -1, -1):
+                    for d in ds:
                         act(send_tip(which, v, h, d))
 
+    groups = [list(range(d, min(d + 2, tmn))) for d in range(0, tmn, 2)]
     for which in range(2):
-        each_near(which, lambda copy: copy.start())
-        for d in range(tmn - 1, 0, -1):
-            send_block(which, d).start()
+        for ds in groups:
+            each_near(which, ds[::-1], lambda copy: copy.start())
+            for d in ds[::-1]:
+                if d:
+                    send_block(which, d).start()
 
     def receive(which, ds, dst):
         for d in ds[ds[0] == 0 :]:
@@ -391,8 +395,6 @@
                 [edge_in[which, s, h].astype(f32) for h in range(2)],
                 [[tip_in[which, s, v, h].astype(f32)[:1] for h in range(2)] for v in range(2)],
             )
-
-    groups = [list(range(d, min(d + 2, tmn))) for d in range(0, tmn, 2)]
 
     for tail in (sx, sc):
         for s in range(tmn):
@@ -456,7 +458,6 @@
         squash = jax.nn.sigmoid(hidden)
         gate[t] = squash * (1.0 + hidden * (1.0 - squash))
         at[(t + 2) * cwp : (t + 3) * cwp, :cells] = tall((hidden * squash).astype(bf))
-    choose_x(groups[-1])
     for k in range(27):
         load_two(k).wait()
 
@@ -552,6 +553,8 @@
     grims = near(grim, gedge, grim_in, gedge_in, gcorner_in, gnear_sem)
     start_all(grims)
 
+    choose_x(groups[-1])
+
     scatter(1)
 
     total = None
@@ -595,14 +598,24 @@
         total = got if total is None else total + got
     back_ref[...] = flat[1] + total[:cells]
 
-    for tensor in (1, 0):
-        acc[tensor] = stage[tensor, col].astype(f32)
+    for tensor, out in ((1, two_ref), (0, one_ref)):
         for z in range(zn):
 
             @pl.when(col != z)
             def _():
                 arrived(landed.at[tensor, z], rs_recv.at[tensor, z])
-                acc[tensor] += landed[tensor, z].astype(f32)
+
+            @pl.when(col == z)
+            def _():
+                landed[tensor, z] = stage[tensor, z]
+
+        got = landed[tensor, 0].astype(f32)
+        for z in range(1, zn):
+            got = got + landed[tensor, z].astype(f32)
+        whole = jnp.concatenate(
+            [got[:, ochunk * q : ochunk * (q + 1)] for q in range(zn)], axis=0
+        ).reshape(slots, chunk_pad, ochunk)
+        out[...] = whole[:27, :chunk, :]
 
     for which in range(2):
         for d in range(1, tmn):
@@ -620,19 +633,17 @@
                 send_piece(which, z).wait_send()
 
     for which in range(2):
-        each_near(which, lambda copy: copy.wait_send())
+        each_near(which, range(tmn), lambda copy: copy.wait_send())
     drain_all(grims)
 
 
-def finish(zn, chunk, chunk_pad, slots, back_ref, acc_ref, out_ref, one_ref, two_ref):
-    ochunk = C // zn
-    out_ref[...] = back_ref[...]
-    for tensor, out in enumerate((one_ref, two_ref)):
-        got = acc_ref[tensor]
-        whole = jnp.concatenate(
-            [got[:, ochunk * q : ochunk * (q + 1)] for q in range(zn)], axis=0
-        ).reshape(slots, chunk_pad, ochunk)
-        out[...] = whole[:27, :chunk, :]
+def finish(back_ref, one_ref, two_ref, back_out, one_out, two_out, sem):
+    pairs = ((back_ref, back_out), (one_ref, one_out), (two_ref, two_out))
+    copies = [pltpu.make_async_copy(src, dst, sem.at[i]) for i, (src, dst) in enumerate(pairs)]
+    for copy in copies:
+        copy.start()
+    for copy in copies:
+        copy.wait()
 
 
 def body(sizes, inputs, cotangent, weight_one, weight_two):
@@ -654,14 +665,16 @@
     group = slots * chunk_pad // zn
     dma = pltpu.SemaphoreType.DMA
     lifted = lift + mp - cells
-    back, acc = pl.pallas_call(
+    sums = (27, chunk, channels // zn)
+    outs = pl.pallas_call(
         functools.partial(kernel, dims),
         out_shape=(
-            jax.ShapeDtypeStruct((cells, channels), f32),
-            jax.ShapeDtypeStruct((2, group, channels), f32),
+            pltpu.VMEM((cells, channels), f32),
+            pltpu.VMEM(sums, f32),
+            pltpu.VMEM(sums, f32),
         ),
         in_specs=[pl.BlockSpec(memory_space=pl.ANY)] * 4,
-        out_specs=(vmem,) * 2,
+        out_specs=(vmem,) * 3,
         scratch_shapes=[
             pltpu.VMEM((2, tmn, cells, channels), bf),
             pltpu.VMEM((2, cells, channels), f32),
@@ -721,15 +734,16 @@
         weight_two.reshape(27 * channels, channels),
     )
     back, one, two = pl.pallas_call(
-        functools.partial(finish, zn, chunk, chunk_pad, slots),
+        finish,
         out_shape=(
             jax.ShapeDtypeStruct((cells, channels), f32),
-            jax.ShapeDtypeStruct((27, chunk, channels // zn), f32),
-            jax.ShapeDtypeStruct((27, chunk, channels // zn), f32),
+            jax.ShapeDtypeStruct(sums, f32),
+            jax.ShapeDtypeStruct(sums, f32),
         ),
-        in_specs=[vmem] * 2,
-        out_specs=(vmem,) * 3,
-    )(back, acc)
+        in_specs=[vmem] * 3,
+        out_specs=(pl.BlockSpec(memory_space=pl.ANY),) * 3,
+        scratch_shapes=[dma((3,))],
+    )(*[pltpu.with_memory_space_constraint(out, pltpu.VMEM) for out in outs])
     return back.reshape(1, rows, cols, channels), one, two
 
 

time: 28.5 us -> 25.8 us (0.905)
  Pallas kernels: 27.6 us -> 24.9 us
    pallas_call x2, Pallas kernels: 27.6 us -> 24.9 us  [the longest x1 24.1 us: body(): pl.pallas_call(functools.partial(kernel, dims), out_shape=(pltpu.VMEM((ce...]
where the time goes in v3:
time: 25.8 us; the launch traced here: 25.6 us
  Pallas kernels  24.9 us (97%)
  between operations  0.64 us (2%)
    pallas_call x1, Pallas kernels, body(): pl.pallas_call(functools.partial(kernel, dims), out_shape=(pltpu.VMEM((ce...  24.1 us
    pallas_call x1, Pallas kernels, body(): pl.pallas_call(finish, out_shape=(jax.ShapeDtypeStruct((cells, channels),...  0.81 us

profile of v3, /device:TPU:0, one launch (start us, length us, event | category | flops | bytes accessed | tf_op | source)
XLA Modules:
  0.0 25.6 jit_solution(7385039129017891824)
XLA Ops:
  0.6 24.1 %shard_map.67 = (f32[136,128]{1,0:T(8,128)S(1)}, f32[27,16,32]{2,1,0:T(8,128)S(1)}, f32[27,16,32]{2,1,0:T(8,128)S(1)}) custom-call(bf16[136,128]{1,0:T(8,128)(2,1)} %bitcast.7, bf16[136,128]{1,0:T(8,128)(2,1)} %bitcast.8, bf16[3456,128]{1,0:T(8,128)(2,1)} %bitcast.5, bf16[3456,128]{1,0:T(8,128)(2,1)} %bitcast.6), custom_call_target="tpu_custom_call" | custom-call | tf_op jit(solution)/shard_map/pallas_call | solution.py:669
  24.8 0.8 %shard_map.68 = (f32[136,128]{1,0:T(8,128)}, f32[27,16,32]{2,1,0:T(8,128)}, f32[27,16,32]{2,1,0:T(8,128)}) custom-call(f32[136,128]{1,0:T(8,128)S(1)} %get-tuple-element.9.back_ref, f32[27,16,32]{2,1,0:T(8,128)S(1)} %get-tuple-element.10.one_ref, f32[27,16,32]{2,1,0:T(8,128)S(1)} %get-tuple-element.11.two_ref), custom_call_target="tpu_custom_call" | custom-call | tf_op jit(solution)/shard_map/pallas_call | solution.py:736

commit v4 on v3

--- a/solution.py
+++ b/solution.py
@@ -57,8 +57,7 @@
     gedge_in,
     gcorner_in,
     own_sem,
-    w1_sem,
-    w2_sem,
+    w_sem,
     blk_send,
     blk_recv,
     near_send,
@@ -85,15 +84,17 @@
     step = (-1, 1)
 
     def partner(d):
-        if tmn == 4:
-            flips = (tm, tm + 1 - 2 * lax.rem(tm, 2), tm + 2 - 4 * (tm // 2), 3 - tm)
-            return flips[d]
-        return lax.rem(tm + d, tmn)
+        got, bit = tm, 1
+        while bit <= d:
+            if d & bit:
+                got = got + bit - 2 * bit * lax.rem(got // bit, 2)
+            bit *= 2
+        return got
 
     blocks = (x_ref, c_ref)
 
     def keep(which):
-        return pltpu.make_async_copy(blocks[which], gat.at[which, tm], own_sem.at[which])
+        return pltpu.make_async_copy(blocks[which], gat.at[which, 0], own_sem.at[which])
 
     keep(0).start()
     keep(1).start()
@@ -141,13 +142,13 @@
     def load_one(k):
         a, q = k // 9, k % 9
         return pltpu.make_async_copy(
-            w1_ref.at[pl.ds(C * k, C), :], r1.at[pl.ds(C * q, C), pl.ds(C * a, C)], w1_sem.at[k]
+            w1_ref.at[pl.ds(C * k, C), :], r1.at[pl.ds(C * q, C), pl.ds(C * a, C)], w_sem.at[0]
         )
 
     def load_two(k):
         a, q = k // 9, k % 9
         return pltpu.make_async_copy(
-            w2_ref.at[pl.ds(C * k, C), :], r2.at[pl.ds(C * a, C), pl.ds(C * q, C)], w2_sem.at[k]
+            w2_ref.at[pl.ds(C * k, C), :], r2.at[pl.ds(C * a, C), pl.ds(C * q, C)], w_sem.at[1]
         )
 
     for k in range(27):
@@ -159,19 +160,19 @@
 
         @pl.when(jnp.logical_not(vert[v]))
         def _():
-            rim_in[:, :, v] = jnp.zeros((2, tmn, cols, C), bf)
-            tip_in[:, :, v] = jnp.zeros((2, tmn, 2, 8, C), bf)
+            rim_in[:, v] = jnp.zeros((2, tmn, cols, C), bf)
+            tip_in[:, v] = jnp.zeros((2, 2, tmn, 8, C), bf)
 
     for h in range(2):
 
         @pl.when(jnp.logical_not(side[h]))
         def _():
-            edge_in[:, :, h] = jnp.zeros((2, tmn, rows, C), bf)
-            tip_in[:, :, :, h] = jnp.zeros((2, tmn, 2, 8, C), bf)
+            edge_in[:, h] = jnp.zeros((2, tmn, rows, C), bf)
+            tip_in[:, :, h] = jnp.zeros((2, 2, tmn, 8, C), bf)
 
     for which in range(2):
         keep(which).wait()
-        flat[which] = gat[which, tm].astype(f32)
+        flat[which] = gat[which, 0].astype(f32)
         for h in range(2):
             edge[which, h] = flat[which, pl.ds(h * (cols - 1), rows, stride=cols), :].astype(bf)
         for v in range(2):
@@ -293,56 +294,58 @@
     nh = side[0].astype(jnp.int32) + side[1].astype(jnp.int32)
     pl.semaphore_wait(barrier, tmn * (1 + nv) * (1 + nh) - 1 + zn - 1 - nh + rn - 1 - nv)
 
+    groups = [list(range(d, min(d + 2, tmn))) for d in range(0, tmn, 2)]
+
     def send_block(which, d):
         return remote(
-            gat.at[which, tm],
-            gat.at[which, tm],
-            blk_send.at[which, d],
-            blk_recv.at[which, tm],
+            gat.at[which, 0],
+            gat.at[which, d],
+            blk_send.at[which],
+            blk_recv.at[which, d // 2],
             (partner(d), row, col),
         )
 
     def send_rim(which, v, d):
         return remote(
             rim.at[which, v],
-            rim_in.at[which, tm, 1 - v],
-            near_send.at[which, v, d],
-            near_recv.at[which, 1 - v, tm],
+            rim_in.at[which, 1 - v, d],
+            near_send.at[v],
+            near_recv.at[which, d // 2, 1 - v],
             (partner(d), row + step[v], col),
         )
 
     def send_edge(which, h, d):
         return remote(
             edge.at[which, h],
-            edge_in.at[which, tm, 1 - h],
-            near_send.at[which, 2 + h, d],
-            near_recv.at[which, 3 - h, tm],
+            edge_in.at[which, 1 - h, d],
+            near_send.at[2 + h],
+            near_recv.at[which, d // 2, 3 - h],
             (partner(d), row, col + step[h]),
         )
 
     def send_tip(which, v, h, d):
         return remote(
             tip.at[which, v, h],
-            tip_in.at[which, tm, 1 - v, 1 - h],
-            near_send.at[which, 4 + 2 * v + h, d],
-            near_recv.at[which, 4 + 2 * (1 - v) + 1 - h, tm],
+            tip_in.at[which, 1 - v, 1 - h, d],
+            near_send.at[4 + 2 * v + h],
+            near_recv.at[which, d // 2, 4 + 2 * (1 - v) + 1 - h],
             (partner(d), row + step[v], col + step[h]),
         )
 
-    def each_near(which, ds, act):
+    def send_near(which, ds):
         for h in range(2):
 
             @pl.when(side[h])
             def _():
                 for d in ds:
-                    act(send_edge(which, h, d))
+                    send_edge(which, h, d).start()
 
         for v in range(2):
 
             @pl.when(vert[v])
             def _():
                 for d in ds:
-                    act(send_rim(which, v, d))
+                    send_rim(which, v, d).start()
 
         for v in range(2):
             for h in range(2):
@@ -350,50 +353,49 @@
                 @pl.when(jnp.logical_and(vert[v], side[h]))
                 def _():
                     for d in ds:
-                        act(send_tip(which, v, h, d))
-
-    groups = [list(range(d, min(d + 2, tmn))) for d in range(0, tmn, 2)]
+                        send_tip(which, v, h, d).start()
+
     for which in range(2):
         for ds in groups:
-            each_near(which, ds[::-1], lambda copy: copy.start())
+            send_near(which, ds[::-1])
             for d in ds[::-1]:
                 if d:
                     send_block(which, d).start()
 
+    def sent(like, sem):
+        remote(like, like, sem, sem, (tm, row, col)).wait_send()
+
     def receive(which, ds, dst):
-        for d in ds[ds[0] == 0 :]:
-            arrived(gat.at[which, partner(d)], blk_recv.at[which, partner(d)])
+        g, span = ds[0] // 2, pl.ds(ds[0], len(ds))
+        if ds[-1]:
+            arrived(gat.at[which, max(ds[0], 1) : ds[-1] + 1], blk_recv.at[which, g])
         for h in range(2):
 
             @pl.when(side[h])
             def _():
-                for d in ds:
-                    arrived(edge_in.at[which, partner(d), h], near_recv.at[which, 2 + h, partner(d)])
+                arrived(edge_in.at[which, h, span], near_recv.at[which, g, 2 + h])
 
         for v in range(2):
 
             @pl.when(vert[v])
             def _():
-                for d in ds:
-                    arrived(rim_in.at[which, partner(d), v], near_recv.at[which, v, partner(d)])
+                arrived(rim_in.at[which, v, span], near_recv.at[which, g, v])
 
         for v in range(2):
             for h in range(2):
 
                 @pl.when(jnp.logical_and(vert[v], side[h]))
                 def _():
-                    for d in ds:
-                        arrived(tip_in.at[which, partner(d), v, h], near_recv.at[which, 4 + 2 * v + h, partner(d)])
+                    arrived(tip_in.at[which, v, h, span], near_recv.at[which, g, 4 + 2 * v + h])
 
         for d in ds:
-            s = partner(d)
             spread(
                 dst.at[d],
-                gat[which, s].astype(f32),
-                rim_in[which, s, 0].astype(f32),
-                rim_in[which, s, 1].astype(f32),
-                [edge_in[which, s, h].astype(f32) for h in range(2)],
-                [[tip_in[which, s, v, h].astype(f32)[:1] for h in range(2)] for v in range(2)],
+                gat[which, d].astype(f32),
+                rim_in[which, 0, d].astype(f32),
+                rim_in[which, 1, d].astype(f32),
+                [edge_in[which, h, d].astype(f32) for h in range(2)],
+                [[tip_in[which, v, h, d].astype(f32)[:1] for h in range(2)] for v in range(2)],
             )
 
     for tail in (sx, sc):
@@ -430,8 +432,11 @@
 
     def choose_x(ds):
         for d in ds:
-            for q in range(9):
-                xt[d, cwp * q : cwp * (q + 1), :mp] = tall(x9[d, :, C * q : C * (q + 1)])
+            for e in range(3):
+                got = lax.dot_general(picked, sx[d, e].astype(bf), NT, preferred_element_type=f32)
+                for b in range(3):
+                    q = 3 * b + e
+                    xt[d, cwp * q : cwp * (q + 1), :mp] = got[:, cols * b : cols * b + mp].astype(bf)
 
     for ds in groups:
         receive(0, ds, sx)
@@ -440,15 +445,12 @@
                 b, e = q // 3, q % 3
                 x9[d, :, C * q : C * (q + 1)] = sx[d, e, cols * b : cols * b + mp, :].astype(bf)
         if ds[0] == 0:
-            for k in range(27):
-                load_one(k).wait()
+            pltpu.make_async_copy(r1, r1, w_sem.at[0]).wait()
         got = jnp.dot(
             x9[ds[0] : ds[-1] + 1].reshape(len(ds) * mp, 9 * C), r1[...], preferred_element_type=f32
         )
         for d in ds:
             conv[partner(d)] = got[(d - ds[0]) * mp : (d - ds[0] + 1) * mp]
-        if ds is not groups[-1]:
-            choose_x(ds)
     for t in range(tmn):
         hidden = conv[t, :cells, 2 * C :]
         for a in range(2):
@@ -458,39 +460,30 @@
         squash = jax.nn.sigmoid(hidden)
         gate[t] = squash * (1.0 + hidden * (1.0 - squash))
         at[(t + 2) * cwp : (t + 3) * cwp, :cells] = tall((hidden * squash).astype(bf))
-    for k in range(27):
-        load_two(k).wait()
-
-    def send_pair(tensor, r):
-        return remote(
-            pstage.at[tensor, r],
-            pland.at[tensor, row],
-            pair_send.at[tensor, r],
-            pair_recv.at[tensor, row],
-            (tm, r, col),
-        )
 
     def send_pairs(tensor):
         for r in range(rn):
 
             @pl.when(row != r)
             def _():
-                send_pair(tensor, r).start()
-
-    def send_piece(tensor, z):
-        return remote(
-            stage.at[tensor, z], landed.at[tensor, col], rs_send.at[tensor, z], rs_recv.at[tensor, col], (tm, row, z)
-        )
+                remote(
+                    pstage.at[tensor, r],
+                    pland.at[tensor, row],
+                    pair_send.at[tensor],
+                    pair_recv.at[tensor],
+                    (tm, r, col),
+                ).start()
 
     group = slots * chunk_pad // zn
 
     def scatter(tensor):
         pp[:taps, :] = part[tensor, row]
+        if rn > 1:
+            arrived(pland.at[tensor, : rn - 1], pair_recv.at[tensor])
         for r in range(rn):
 
             @pl.when(row != r)
             def _():
-                arrived(pland.at[tensor, r], pair_recv.at[tensor, r])
                 pp[:taps, :] += pland[tensor, r].astype(f32)
 
         for z in range(zn):
@@ -502,7 +495,13 @@
 
             @pl.when(col != z)
             def _():
-                send_piece(tensor, z).start()
+                remote(
+                    stage.at[tensor, z],
+                    landed.at[tensor, col],
+                    rs_send.at[tensor],
+                    rs_recv.at[tensor],
+                    (tm, row, z),
+                ).start()
 
     total = None
     for ds in groups:
@@ -515,20 +514,21 @@
             lines = pl.ds(pl.multiple_of(partner(d) * cwp, 16), 3 * cwp)
             got = jnp.dot(at[lines, :], c9[d], preferred_element_type=f32)
             total = got if total is None else total + got
-        if ds is groups[-1]:
-            for a in range(3):
-                for r in range(rn):
-                    for q in range(9):
-                        k = 9 * a + q
-                        piece = total[a * cwp + r * chunk_pad : a * cwp + (r + 1) * chunk_pad, C * q : C * (q + 1)]
-                        part[1, r, k * chunk_pad : (k + 1) * chunk_pad, :] = piece
-                        pstage[1, r, k * chunk_pad : (k + 1) * chunk_pad, :] = piece.astype(bf)
-            send_pairs(1)
-        got = lax.dot_general(
-            c9[ds[0] : ds[-1] + 1, :mp, :].reshape(len(ds) * mp, 9 * C), r2[...], NT, preferred_element_type=f32
-        )
-        for d in ds:
-            conv[partner(d)] = got[(d - ds[0]) * mp : (d - ds[0] + 1) * mp]
+    for a in range(3):
+        for r in range(rn):
+            for q in range(9):
+                k = 9 * a + q
+                piece = total[a * cwp + r * chunk_pad : a * cwp + (r + 1) * chunk_pad, C * q : C * (q + 1)]
+                part[1, r, k * chunk_pad : (k + 1) * chunk_pad, :] = piece
+                pstage[1, r, k * chunk_pad : (k + 1) * chunk_pad, :] = piece.astype(bf)
+    send_pairs(1)
+
+    pltpu.make_async_copy(r2, r2, w_sem.at[1]).wait()
+    got = lax.dot_general(
+        c9[:, :mp, :].reshape(tmn * mp, 9 * C), r2[...], NT, preferred_element_type=f32
+    )
+    for d in range(tmn):
+        conv[partner(d)] = got[d * mp : (d + 1) * mp]
     for t in range(tmn):
         grad = conv[t, :cells, 2 * C :]
         for a in range(2):
@@ -553,7 +553,7 @@
     grims = near(grim, gedge, grim_in, gedge_in, gcorner_in, gnear_sem)
     start_all(grims)
 
-    choose_x(groups[-1])
+    choose_x(range(tmn))
 
     scatter(1)
 
@@ -599,16 +599,9 @@
     back_ref[...] = flat[1] + total[:cells]
 
     for tensor, out in ((1, two_ref), (0, one_ref)):
-        for z in range(zn):
-
-            @pl.when(col != z)
-            def _():
-                arrived(landed.at[tensor, z], rs_recv.at[tensor, z])
-
-            @pl.when(col == z)
-            def _():
-                landed[tensor, z] = stage[tensor, z]
-
+        landed[tensor, col] = stage[tensor, col]
+        if zn > 1:
+            arrived(landed.at[tensor, : zn - 1], rs_recv.at[tensor])
         got = landed[tensor, 0].astype(f32)
         for z in range(1, zn):
             got = got + landed[tensor, z].astype(f32)
@@ -618,22 +611,31 @@
         out[...] = whole[:27, :chunk, :]
 
     for which in range(2):
-        for d in range(1, tmn):
-            send_block(which, d).wait_send()
-        for r in range(rn):
-
-            @pl.when(row != r)
-            def _():
-                send_pair(which, r).wait_send()
-
-        for z in range(zn):
-
-            @pl.when(col != z)
-            def _():
-                send_piece(which, z).wait_send()
-
-    for which in range(2):
-        each_near(which, range(tmn), lambda copy: copy.wait_send())
+        if tmn > 1:
+            sent(gat.at[which, 1:], blk_send.at[which])
+        if rn > 1:
+            sent(pstage.at[which, : rn - 1], pair_send.at[which])
+        if zn > 1:
+            sent(stage.at[which, : zn - 1], rs_send.at[which])
+    for h in range(2):
+
+        @pl.when(side[h])
+        def _():
+            sent(edge_in.at[:, h], near_send.at[2 + h])
+
+    for v in range(2):
+
+        @pl.when(vert[v])
+        def _():
+            sent(rim_in.at[:, v], near_send.at[v])
+
+    for v in range(2):
+        for h in range(2):
+
+            @pl.when(jnp.logical_and(vert[v], side[h]))
+            def _():
+                sent(tip_in.at[:, v, h], near_send.at[4 + 2 * v + h])
+
     drain_all(grims)
 
 
@@ -703,26 +705,25 @@
             pltpu.VMEM((2, 2, cols, channels), bf),
             pltpu.VMEM((2, 2, rows, channels), bf),
             pltpu.VMEM((2, 2, 2, 8, channels), bf),
-            pltpu.VMEM((2, tmn, 2, cols, channels), bf),
-            pltpu.VMEM((2, tmn, 2, rows, channels), bf),
-            pltpu.VMEM((2, tmn, 2, 2, 8, channels), bf),
+            pltpu.VMEM((2, 2, tmn, cols, channels), bf),
+            pltpu.VMEM((2, 2, tmn, rows, channels), bf),
+            pltpu.VMEM((2, 2, 2, tmn, 8, channels), bf),
             pltpu.VMEM((2, 3 * cols, channels), bf),
             pltpu.VMEM((2, 3 * rows, channels), bf),
             pltpu.VMEM((2, 3 * cols, channels), bf),
             pltpu.VMEM((2, 3 * rows, channels), bf),
             pltpu.VMEM((2, 2, 3 * rows, channels), bf),
             dma((2,)),
-            dma((27,)),
-            dma((27,)),
-            dma((2, tmn)),
-            dma((2, tmn)),
-            dma((2, 8, tmn)),
-            dma((2, 8, tmn)),
+            dma((2,)),
+            dma((2,)),
+            dma((2, -(-tmn // 2))),
+            dma((8,)),
+            dma((2, -(-tmn // 2), 8)),
             dma((2, 8)),
-            dma((2, rn)),
-            dma((2, rn)),
-            dma((2, zn)),
-            dma((2, zn)),
+            dma((2,)),
+            dma((2,)),
+            dma((2,)),
+            dma((2,)),
         ],
         compiler_params=pltpu.CompilerParams(
             collective_id=0, has_side_effects=True, vmem_limit_bytes=60 * 1024 * 1024

time: 25.8 us -> 23.8 us (0.922)
  Pallas kernels: 24.9 us -> 22.9 us
    pallas_call x1, Pallas kernels: 24.1 us -> 22.1 us  [body(): pl.pallas_call(functools.partial(kernel, dims), out_shape=(pltpu.VMEM((ce...]
where the time goes in v4:
time: 23.8 us; the launch traced here: 23.6 us
  Pallas kernels  22.9 us (96%)
  between operations  0.64 us (3%)
    pallas_call x1, Pallas kernels, body(): pl.pallas_call(functools.partial(kernel, dims), out_shape=(pltpu.VMEM((ce...  22.1 us
    pallas_call x1, Pallas kernels, body(): pl.pallas_call(finish, out_shape=(jax.ShapeDtypeStruct((cells, channels),...  0.81 us

profile of v4, /device:TPU:0, one launch (start us, length us, event | category | flops | bytes accessed | tf_op | source)
XLA Modules:
  0.0 23.6 jit_solution(12616190526225946767)
XLA Ops:
  0.6 22.1 %shard_map.67 = (f32[136,128]{1,0:T(8,128)S(1)}, f32[27,16,32]{2,1,0:T(8,128)S(1)}, f32[27,16,32]{2,1,0:T(8,128)S(1)}) custom-call(bf16[136,128]{1,0:T(8,128)(2,1)} %bitcast.7, bf16[136,128]{1,0:T(8,128)(2,1)} %bitcast.8, bf16[3456,128]{1,0:T(8,128)(2,1)} %bitcast.5, bf16[3456,128]{1,0:T(8,128)(2,1)} %bitcast.6), custom_call_target="tpu_custom_call" | custom-call | tf_op jit(solution)/shard_map/pallas_call | solution.py:671
  22.8 0.8 %shard_map.68 = (f32[136,128]{1,0:T(8,128)}, f32[27,16,32]{2,1,0:T(8,128)}, f32[27,16,32]{2,1,0:T(8,128)}) custom-call(f32[136,128]{1,0:T(8,128)S(1)} %get-tuple-element.9.back_ref, f32[27,16,32]{2,1,0:T(8,128)S(1)} %get-tuple-element.10.one_ref, f32[27,16,32]{2,1,0:T(8,128)S(1)} %get-tuple-element.11.two_ref), custom_call_target="tpu_custom_call" | custom-call | tf_op jit(solution)/shard_map/pallas_call | solution.py:737

commit v5 on v4

--- a/solution.py
+++ b/solution.py
@@ -62,6 +62,7 @@
     blk_recv,
     near_send,
     near_recv,
+    told,
     gnear_sem,
     pair_send,
     pair_recv,
@@ -103,35 +104,20 @@
     def greet(place):
         pl.semaphore_signal(barrier, inc=1, device_id=place, device_id_type=MESH)
 
-    for z in range(zn):
-
-        @pl.when(jnp.logical_or(col - z > 1, z - col > 1))
-        def _():
-            greet((tm, row, z))
-
     for d in range(tmn - 1, 0, -1):
         greet((partner(d), row, col))
-    for v in range(2):
-        for h in range(2):
-
-            @pl.when(jnp.logical_and(vert[v], side[h]))
-            def _():
-                for d in range(tmn - 1, -1, -1):
-                    greet((partner(d), row + step[v], col + step[h]))
-
-    for h in range(2):
-
-        @pl.when(side[h])
-        def _():
-            for d in range(tmn - 1, -1, -1):
-                greet((partner(d), row, col + step[h]))
-
     for v in range(2):
 
         @pl.when(vert[v])
         def _():
             for d in range(tmn - 1, -1, -1):
                 greet((partner(d), row + step[v], col))
+
+    for h in range(2):
+
+        @pl.when(side[h])
+        def _():
+            greet((tm, row, col + step[h]))
 
     for r in range(rn if rn > 2 else 0):
 
@@ -292,7 +278,25 @@
 
     nv = vert[0].astype(jnp.int32) + vert[1].astype(jnp.int32)
     nh = side[0].astype(jnp.int32) + side[1].astype(jnp.int32)
-    pl.semaphore_wait(barrier, tmn * (1 + nv) * (1 + nh) - 1 + zn - 1 - nh + rn - 1 - nv)
+    pl.semaphore_wait(barrier, tmn * (1 + nv) - 1 + nh + rn - 1 - nv)
+
+    def tell():
+        for h in range(2):
+
+            @pl.when(side[h])
+            def _():
+                pl.semaphore_signal(
+                    told.at[1 - h], inc=1, device_id=(tm, row, col + step[h]), device_id_type=MESH
+                )
+
+    def hear():
+        for h in range(2):
+
+            @pl.when(side[h])
+            def _():
+                pl.semaphore_wait(told.at[h], 1)
+
+    tell()
 
     groups = [list(range(d, min(d + 2, tmn))) for d in range(0, tmn, 2)]
 
@@ -355,12 +359,17 @@
                     for d in ds:
                         send_tip(which, v, h, d).start()
 
-    for which in range(2):
-        for ds in groups:
-            send_near(which, ds[::-1])
-            for d in ds[::-1]:
-                if d:
-                    send_block(which, d).start()
+    for d in range(1, tmn):
+        send_block(0, d).start()
+    hear()
+    tell()
+    for ds in groups:
+        send_near(0, ds[::-1])
+    for ds in groups:
+        send_near(1, ds[::-1])
+        for d in ds[::-1]:
+            if d:
+                send_block(1, d).start()
 
     def sent(like, sem):
         remote(like, like, sem, sem, (tm, row, col)).wait_send()
@@ -451,6 +460,8 @@
         )
         for d in ds:
             conv[partner(d)] = got[(d - ds[0]) * mp : (d - ds[0] + 1) * mp]
+        if ds is not groups[-1]:
+            choose_x(ds)
     for t in range(tmn):
         hidden = conv[t, :cells, 2 * C :]
         for a in range(2):
@@ -523,12 +534,19 @@
                 pstage[1, r, k * chunk_pad : (k + 1) * chunk_pad, :] = piece.astype(bf)
     send_pairs(1)
 
+    for _ in range(max(0, zn - 4)):
+        hear()
+        tell()
+    hear()
+
     pltpu.make_async_copy(r2, r2, w_sem.at[1]).wait()
     got = lax.dot_general(
         c9[:, :mp, :].reshape(tmn * mp, 9 * C), r2[...], NT, preferred_element_type=f32
     )
     for d in range(tmn):
         conv[partner(d)] = got[d * mp : (d + 1) * mp]
+    scatter(1)
+
     for t in range(tmn):
         grad = conv[t, :cells, 2 * C :]
         for a in range(2):
@@ -553,9 +571,7 @@
     grims = near(grim, gedge, grim_in, gedge_in, gcorner_in, gnear_sem)
     start_all(grims)
 
-    choose_x(range(tmn))
-
-    scatter(1)
+    choose_x(groups[-1])
 
     total = None
     for d in range(tmn):
@@ -719,6 +735,7 @@
             dma((2, -(-tmn // 2))),
             dma((8,)),
             dma((2, -(-tmn // 2), 8)),
+            pltpu.SemaphoreType.REGULAR((2,)),
             dma((2, 8)),
             dma((2,)),
             dma((2,)),

time: 23.8 us -> 24 us (level)
  Pallas kernels: 22.9 us -> 23.2 us
where the time goes in v5:
time: 24 us; the launch traced here: 23.8 us
  Pallas kernels  23.2 us (97%)
  between operations  0.64 us (3%)
    pallas_call x1, Pallas kernels, body(): pl.pallas_call(functools.partial(kernel, dims), out_shape=(pltpu.VMEM((ce...  22.3 us
    pallas_call x1, Pallas kernels, body(): pl.pallas_call(finish, out_shape=(jax.ShapeDtypeStruct((cells, channels),...  0.81 us

profile of v5, /device:TPU:0, one launch (start us, length us, event | category | flops | bytes accessed | tf_op | source)
XLA Modules:
  0.0 23.8 jit_solution(13431202150786607391)
XLA Ops:
  0.6 22.3 %shard_map.67 = (f32[136,128]{1,0:T(8,128)S(1)}, f32[27,16,32]{2,1,0:T(8,128)S(1)}, f32[27,16,32]{2,1,0:T(8,128)S(1)}) custom-call(bf16[136,128]{1,0:T(8,128)(2,1)} %bitcast.7, bf16[136,128]{1,0:T(8,128)(2,1)} %bitcast.8, bf16[3456,128]{1,0:T(8,128)(2,1)} %bitcast.5, bf16[3456,128]{1,0:T(8,128)(2,1)} %bitcast.6), custom_call_target="tpu_custom_call" | custom-call | tf_op jit(solution)/shard_map/pallas_call | solution.py:687
  23.0 0.8 %shard_map.68 = (f32[136,128]{1,0:T(8,128)}, f32[27,16,32]{2,1,0:T(8,128)}, f32[27,16,32]{2,1,0:T(8,128)}) custom-call(f32[136,128]{1,0:T(8,128)S(1)} %get-tuple-element.9.back_ref, f32[27,16,32]{2,1,0:T(8,128)S(1)} %get-tuple-element.10.one_ref, f32[27,16,32]{2,1,0:T(8,128)S(1)} %get-tuple-element.11.two_ref), custom_call_target="tpu_custom_call" | custom-call | tf_op jit(solution)/shard_map/pallas_call | solution.py:754

commit v6 on v4

--- a/solution.py
+++ b/solution.py
@@ -103,21 +103,14 @@
     def greet(place):
         pl.semaphore_signal(barrier, inc=1, device_id=place, device_id_type=MESH)
 
-    for z in range(zn):
-
-        @pl.when(jnp.logical_or(col - z > 1, z - col > 1))
-        def _():
-            greet((tm, row, z))
-
     for d in range(tmn - 1, 0, -1):
         greet((partner(d), row, col))
     for v in range(2):
-        for h in range(2):
-
-            @pl.when(jnp.logical_and(vert[v], side[h]))
-            def _():
-                for d in range(tmn - 1, -1, -1):
-                    greet((partner(d), row + step[v], col + step[h]))
+
+        @pl.when(vert[v])
+        def _():
+            for d in range(tmn - 1, -1, -1):
+                greet((partner(d), row + step[v], col))
 
     for h in range(2):
 
@@ -127,11 +120,18 @@
                 greet((partner(d), row, col + step[h]))
 
     for v in range(2):
-
-        @pl.when(vert[v])
+        for h in range(2):
+
+            @pl.when(jnp.logical_and(vert[v], side[h]))
+            def _():
+                for d in range(tmn - 1, -1, -1):
+                    greet((partner(d), row + step[v], col + step[h]))
+
+    for z in range(zn):
+
+        @pl.when(jnp.logical_or(col - z > 1, z - col > 1))
         def _():
-            for d in range(tmn - 1, -1, -1):
-                greet((partner(d), row + step[v], col))
+            greet((tm, row, z))
 
     for r in range(rn if rn > 2 else 0):
 
@@ -310,7 +310,7 @@
             rim.at[which, v],
             rim_in.at[which, 1 - v, d],
             near_send.at[v],
-            near_recv.at[which, d // 2, 1 - v],
+            near_recv.at[which, 1 - v],
             (partner(d), row + step[v], col),
         )
 
@@ -319,7 +319,7 @@
             edge.at[which, h],
             edge_in.at[which, 1 - h, d],
             near_send.at[2 + h],
-            near_recv.at[which, d // 2, 3 - h],
+            near_recv.at[which, 3 - h],
             (partner(d), row, col + step[h]),
         )
 
@@ -328,7 +328,7 @@
             tip.at[which, v, h],
             tip_in.at[which, 1 - v, 1 - h, d],
             near_send.at[4 + 2 * v + h],
-            near_recv.at[which, d // 2, 4 + 2 * (1 - v) + 1 - h],
+            near_recv.at[which, 4 + 2 * (1 - v) + 1 - h],
             (partner(d), row + step[v], col + step[h]),
         )
 
@@ -356,8 +356,8 @@
                         send_tip(which, v, h, d).start()
 
     for which in range(2):
+        send_near(which, range(tmn - 1, -1, -1))
         for ds in groups:
-            send_near(which, ds[::-1])
             for d in ds[::-1]:
                 if d:
                     send_block(which, d).start()
@@ -366,27 +366,27 @@
         remote(like, like, sem, sem, (tm, row, col)).wait_send()
 
     def receive(which, ds, dst):
-        g, span = ds[0] // 2, pl.ds(ds[0], len(ds))
+        g = ds[0] // 2
         if ds[-1]:
             arrived(gat.at[which, max(ds[0], 1) : ds[-1] + 1], blk_recv.at[which, g])
-        for h in range(2):
+        for h in range(2 if g == 0 else 0):
 
             @pl.when(side[h])
             def _():
-                arrived(edge_in.at[which, h, span], near_recv.at[which, g, 2 + h])
-
-        for v in range(2):
+                arrived(edge_in.at[which, h], near_recv.at[which, 2 + h])
+
+        for v in range(2 if g == 0 else 0):
 
             @pl.when(vert[v])
             def _():
-                arrived(rim_in.at[which, v, span], near_recv.at[which, g, v])
-
-        for v in range(2):
+                arrived(rim_in.at[which, v], near_recv.at[which, v])
+
+        for v in range(2 if g == 0 else 0):
             for h in range(2):
 
                 @pl.when(jnp.logical_and(vert[v], side[h]))
                 def _():
-                    arrived(tip_in.at[which, v, h, span], near_recv.at[which, g, 4 + 2 * v + h])
+                    arrived(tip_in.at[which, v, h], near_recv.at[which, 4 + 2 * v + h])
 
         for d in ds:
             spread(
@@ -451,6 +451,8 @@
         )
         for d in ds:
             conv[partner(d)] = got[(d - ds[0]) * mp : (d - ds[0] + 1) * mp]
+        if ds is not groups[-1]:
+            choose_x(ds)
     for t in range(tmn):
         hidden = conv[t, :cells, 2 * C :]
         for a in range(2):
@@ -491,7 +493,6 @@
                 [pp[group * q : group * (q + 1), ochunk * z : ochunk * (z + 1)] for q in range(zn)],
                 axis=1,
             ).astype(bf)
-        for z in range(zn):
 
             @pl.when(col != z)
             def _():
@@ -512,7 +513,7 @@
                 c9[d, :mp, C * q : C * (q + 1)] = sc[d, 2 - e, cols * (2 - b) : cols * (2 - b) + mp, :].astype(bf)
         for d in ds:
             lines = pl.ds(pl.multiple_of(partner(d) * cwp, 16), 3 * cwp)
-            got = jnp.dot(at[lines, :], c9[d], preferred_element_type=f32)
+            got = jnp.dot(at[lines, :mp], c9[d, :mp], preferred_element_type=f32)
             total = got if total is None else total + got
     for a in range(3):
         for r in range(rn):
@@ -553,15 +554,15 @@
     grims = near(grim, gedge, grim_in, gedge_in, gcorner_in, gnear_sem)
     start_all(grims)
 
-    choose_x(range(tmn))
-
     scatter(1)
+
+    choose_x(groups[-1])
 
     total = None
     for d in range(tmn):
         s = partner(d)
-        right_side = jnp.concatenate([ghb[s + 2], ghb[s + 1], ghb[s]], axis=1)
-        got = jnp.dot(xt[d], right_side, preferred_element_type=f32)
+        right_side = jnp.concatenate([ghb[s + 2, :mp], ghb[s + 1, :mp], ghb[s, :mp]], axis=1)
+        got = jnp.dot(xt[d, :, :mp], right_side, preferred_element_type=f32)
         total = got if total is None else total + got
     for q in range(9):
         for r in range(rn):
@@ -718,7 +719,7 @@
             dma((2,)),
             dma((2, -(-tmn // 2))),
             dma((8,)),
-            dma((2, -(-tmn // 2), 8)),
+            dma((2, 8)),
             dma((2, 8)),
             dma((2,)),
             dma((2,)),

time: 23.8 us -> 23.4 us (0.983)
  Pallas kernels: 22.9 us -> 22.6 us
    pallas_call x1, Pallas kernels: 22.1 us -> 21.8 us  [body(): pl.pallas_call(functools.partial(kernel, dims), out_shape=(pltpu.VMEM((ce...]
where the time goes in v6:
time: 23.4 us; the launch traced here: 23.2 us
  Pallas kernels  22.6 us (97%)
  between operations  0.64 us (3%)
    pallas_call x1, Pallas kernels, body(): pl.pallas_call(functools.partial(kernel, dims), out_shape=(pltpu.VMEM((ce...  21.8 us
    pallas_call x1, Pallas kernels, body(): pl.pallas_call(finish, out_shape=(jax.ShapeDtypeStruct((cells, channels),...  0.81 us

profile of v6, /device:TPU:0, one launch (start us, length us, event | category | flops | bytes accessed | tf_op | source)
XLA Modules:
  0.0 23.2 jit_solution(2708850029754805054)
XLA Ops:
  0.6 21.8 %shard_map.67 = (f32[136,128]{1,0:T(8,128)S(1)}, f32[27,16,32]{2,1,0:T(8,128)S(1)}, f32[27,16,32]{2,1,0:T(8,128)S(1)}) custom-call(bf16[136,128]{1,0:T(8,128)(2,1)} %bitcast.7, bf16[136,128]{1,0:T(8,128)(2,1)} %bitcast.8, bf16[3456,128]{1,0:T(8,128)(2,1)} %bitcast.5, bf16[3456,128]{1,0:T(8,128)(2,1)} %bitcast.6), custom_call_target="tpu_custom_call" | custom-call | tf_op jit(solution)/shard_map/pallas_call | solution.py:672
  22.4 0.8 %shard_map.68 = (f32[136,128]{1,0:T(8,128)}, f32[27,16,32]{2,1,0:T(8,128)}, f32[27,16,32]{2,1,0:T(8,128)}) custom-call(f32[136,128]{1,0:T(8,128)S(1)} %get-tuple-element.9.back_ref, f32[27,16,32]{2,1,0:T(8,128)S(1)} %get-tuple-element.10.one_ref, f32[27,16,32]{2,1,0:T(8,128)S(1)} %get-tuple-element.11.two_ref), custom_call_target="tpu_custom_call" | custom-call | tf_op jit(solution)/shard_map/pallas_call | solution.py:738

commit v7 on v6

--- a/solution.py
+++ b/solution.py
@@ -451,8 +451,6 @@
         )
         for d in ds:
             conv[partner(d)] = got[(d - ds[0]) * mp : (d - ds[0] + 1) * mp]
-        if ds is not groups[-1]:
-            choose_x(ds)
     for t in range(tmn):
         hidden = conv[t, :cells, 2 * C :]
         for a in range(2):
@@ -463,46 +461,40 @@
         gate[t] = squash * (1.0 + hidden * (1.0 - squash))
         at[(t + 2) * cwp : (t + 3) * cwp, :cells] = tall((hidden * squash).astype(bf))
 
-    def send_pairs(tensor):
-        for r in range(rn):
-
-            @pl.when(row != r)
-            def _():
-                remote(
-                    pstage.at[tensor, r],
-                    pland.at[tensor, row],
-                    pair_send.at[tensor],
-                    pair_recv.at[tensor],
-                    (tm, r, col),
-                ).start()
+    def send_pairs(tensor, lo, hi):
+        for d in range(1, rn):
+            r = lax.rem(row + d, rn)
+            remote(
+                pstage.at[tensor, r, lo:hi],
+                pland.at[tensor, row, lo:hi],
+                pair_send.at[tensor],
+                pair_recv.at[tensor],
+                (tm, r, col),
+            ).start()
 
     group = slots * chunk_pad // zn
 
     def scatter(tensor):
-        pp[:taps, :] = part[tensor, row]
         if rn > 1:
             arrived(pland.at[tensor, : rn - 1], pair_recv.at[tensor])
-        for r in range(rn):
-
-            @pl.when(row != r)
-            def _():
-                pp[:taps, :] += pland[tensor, r].astype(f32)
-
+        got = part[tensor, row]
+        for d in range(1, rn):
+            got = got + pland[tensor, lax.rem(row + d, rn)].astype(f32)
+        pp[:taps, :] = got
         for z in range(zn):
             stage[tensor, z] = jnp.concatenate(
                 [pp[group * q : group * (q + 1), ochunk * z : ochunk * (z + 1)] for q in range(zn)],
                 axis=1,
             ).astype(bf)
-
-            @pl.when(col != z)
-            def _():
-                remote(
-                    stage.at[tensor, z],
-                    landed.at[tensor, col],
-                    rs_send.at[tensor],
-                    rs_recv.at[tensor],
-                    (tm, row, z),
-                ).start()
+        for d in range(1, zn):
+            z = lax.rem(col + d, zn)
+            remote(
+                stage.at[tensor, z],
+                landed.at[tensor, col],
+                rs_send.at[tensor],
+                rs_recv.at[tensor],
+                (tm, row, z),
+            ).start()
 
     total = None
     for ds in groups:
@@ -522,7 +514,7 @@
                 piece = total[a * cwp + r * chunk_pad : a * cwp + (r + 1) * chunk_pad, C * q : C * (q + 1)]
                 part[1, r, k * chunk_pad : (k + 1) * chunk_pad, :] = piece
                 pstage[1, r, k * chunk_pad : (k + 1) * chunk_pad, :] = piece.astype(bf)
-    send_pairs(1)
+    send_pairs(1, 0, taps)
 
     pltpu.make_async_copy(r2, r2, w_sem.at[1]).wait()
     got = lax.dot_general(
@@ -556,22 +548,24 @@
 
     scatter(1)
 
-    choose_x(groups[-1])
-
-    total = None
-    for d in range(tmn):
-        s = partner(d)
-        right_side = jnp.concatenate([ghb[s + 2, :mp], ghb[s + 1, :mp], ghb[s, :mp]], axis=1)
-        got = jnp.dot(xt[d, :, :mp], right_side, preferred_element_type=f32)
-        total = got if total is None else total + got
-    for q in range(9):
-        for r in range(rn):
-            for a in range(3):
-                k = 9 * a + q
-                piece = total[q * cwp + r * chunk_pad : q * cwp + (r + 1) * chunk_pad, C * a : C * (a + 1)]
-                part[0, r, k * chunk_pad : (k + 1) * chunk_pad, :] = piece
-                pstage[0, r, k * chunk_pad : (k + 1) * chunk_pad, :] = piece.astype(bf)
-    send_pairs(0)
+    choose_x(range(tmn))
+
+    for lo, hi in ((0, 2), (2, 3)):
+        total = None
+        for d in range(tmn):
+            s = partner(d)
+            right_side = jnp.concatenate([ghb[s + 2 - a, :mp] for a in range(lo, hi)], axis=1)
+            got = jnp.dot(xt[d, :, :mp], right_side, preferred_element_type=f32)
+            total = got if total is None else total + got
+        for a in range(lo, hi):
+            for r in range(rn):
+                for q in range(9):
+                    k = 9 * a + q
+                    base = q * cwp + r * chunk_pad
+                    piece = total[base : base + chunk_pad, C * (a - lo) : C * (a - lo + 1)]
+                    part[0, r, k * chunk_pad : (k + 1) * chunk_pad, :] = piece
+                    pstage[0, r, k * chunk_pad : (k + 1) * chunk_pad, :] = piece.astype(bf)
+        send_pairs(0, 9 * lo * chunk_pad, 9 * hi * chunk_pad)
 
     scatter(0)
 

time: 23.4 us -> 23.5 us (level)
  no operation moved by 1% of the time
where the time goes in v7:
time: 23.5 us; the launch traced here: 23.3 us
  Pallas kernels  22.7 us (97%)
  between operations  0.64 us (3%)
    pallas_call x1, Pallas kernels, body(): pl.pallas_call(functools.partial(kernel, dims), out_shape=(pltpu.VMEM((ce...  21.9 us
    pallas_call x1, Pallas kernels, body(): pl.pallas_call(finish, out_shape=(jax.ShapeDtypeStruct((cells, channels),...  0.81 us

profile of v7, /device:TPU:0, one launch (start us, length us, event | category | flops | bytes accessed | tf_op | source)
XLA Modules:
  0.0 23.3 jit_solution(18048642258258406540)
XLA Ops:
  0.6 21.9 %shard_map.67 = (f32[136,128]{1,0:T(8,128)S(1)}, f32[27,16,32]{2,1,0:T(8,128)S(1)}, f32[27,16,32]{2,1,0:T(8,128)S(1)}) custom-call(bf16[136,128]{1,0:T(8,128)(2,1)} %bitcast.7, bf16[136,128]{1,0:T(8,128)(2,1)} %bitcast.8, bf16[3456,128]{1,0:T(8,128)(2,1)} %bitcast.5, bf16[3456,128]{1,0:T(8,128)(2,1)} %bitcast.6), custom_call_target="tpu_custom_call" | custom-call | tf_op jit(solution)/shard_map/pallas_call | solution.py:666
  22.5 0.8 %shard_map.68 = (f32[136,128]{1,0:T(8,128)}, f32[27,16,32]{2,1,0:T(8,128)}, f32[27,16,32]{2,1,0:T(8,128)}) custom-call(f32[136,128]{1,0:T(8,128)S(1)} %get-tuple-element.9.back_ref, f32[27,16,32]{2,1,0:T(8,128)S(1)} %get-tuple-element.10.one_ref, f32[27,16,32]{2,1,0:T(8,128)S(1)} %get-tuple-element.11.two_ref), custom_call_target="tpu_custom_call" | custom-call | tf_op jit(solution)/shard_map/pallas_call | solution.py:732

commit v8 on v7

--- a/solution.py
+++ b/solution.py
@@ -451,6 +451,8 @@
         )
         for d in ds:
             conv[partner(d)] = got[(d - ds[0]) * mp : (d - ds[0] + 1) * mp]
+        if ds is not groups[-1]:
+            choose_x(ds)
     for t in range(tmn):
         hidden = conv[t, :cells, 2 * C :]
         for a in range(2):
@@ -461,12 +463,12 @@
         gate[t] = squash * (1.0 + hidden * (1.0 - squash))
         at[(t + 2) * cwp : (t + 3) * cwp, :cells] = tall((hidden * squash).astype(bf))
 
-    def send_pairs(tensor, lo, hi):
+    def send_pairs(tensor):
         for d in range(1, rn):
             r = lax.rem(row + d, rn)
             remote(
-                pstage.at[tensor, r, lo:hi],
-                pland.at[tensor, row, lo:hi],
+                pstage.at[tensor, r],
+                pland.at[tensor, row],
                 pair_send.at[tensor],
                 pair_recv.at[tensor],
                 (tm, r, col),
@@ -514,7 +516,7 @@
                 piece = total[a * cwp + r * chunk_pad : a * cwp + (r + 1) * chunk_pad, C * q : C * (q + 1)]
                 part[1, r, k * chunk_pad : (k + 1) * chunk_pad, :] = piece
                 pstage[1, r, k * chunk_pad : (k + 1) * chunk_pad, :] = piece.astype(bf)
-    send_pairs(1, 0, taps)
+    send_pairs(1)
 
     pltpu.make_async_copy(r2, r2, w_sem.at[1]).wait()
     got = lax.dot_general(
@@ -548,24 +550,22 @@
 
     scatter(1)
 
-    choose_x(range(tmn))
-
-    for lo, hi in ((0, 2), (2, 3)):
-        total = None
-        for d in range(tmn):
-            s = partner(d)
-            right_side = jnp.concatenate([ghb[s + 2 - a, :mp] for a in range(lo, hi)], axis=1)
-            got = jnp.dot(xt[d, :, :mp], right_side, preferred_element_type=f32)
-            total = got if total is None else total + got
-        for a in range(lo, hi):
-            for r in range(rn):
-                for q in range(9):
-                    k = 9 * a + q
-                    base = q * cwp + r * chunk_pad
-                    piece = total[base : base + chunk_pad, C * (a - lo) : C * (a - lo + 1)]
-                    part[0, r, k * chunk_pad : (k + 1) * chunk_pad, :] = piece
-                    pstage[0, r, k * chunk_pad : (k + 1) * chunk_pad, :] = piece.astype(bf)
-        send_pairs(0, 9 * lo * chunk_pad, 9 * hi * chunk_pad)
+    choose_x(groups[-1])
+
+    total = None
+    for d in range(tmn):
+        s = partner(d)
+        right_side = jnp.concatenate([ghb[s + 2 - a, :mp] for a in range(3)], axis=1)
+        got = jnp.dot(xt[d, :, :mp], right_side, preferred_element_type=f32)
+        total = got if total is None else total + got
+    for q in range(9):
+        for r in range(rn):
+            for a in range(3):
+                k = 9 * a + q
+                piece = total[q * cwp + r * chunk_pad : q * cwp + (r + 1) * chunk_pad, C * a : C * (a + 1)]
+                part[0, r, k * chunk_pad : (k + 1) * chunk_pad, :] = piece
+                pstage[0, r, k * chunk_pad : (k + 1) * chunk_pad, :] = piece.astype(bf)
+    send_pairs(0)
 
     scatter(0)
 

time: 23.5 us -> 23.5 us (level)
  no operation moved by 1% of the time
where the time goes in v8:
time: 23.5 us; the launch traced here: 23.3 us
  Pallas kernels  22.6 us (96%)
  between operations  0.64 us (3%)
    pallas_call x1, Pallas kernels, body(): pl.pallas_call(functools.partial(kernel, dims), out_shape=(pltpu.VMEM((ce...  21.8 us
    pallas_call x1, Pallas kernels, body(): pl.pallas_call(finish, out_shape=(jax.ShapeDtypeStruct((cells, channels),...  0.81 us

profile of v8, /device:TPU:0, one launch (start us, length us, event | category | flops | bytes accessed | tf_op | source)
XLA Modules:
  0.0 23.3 jit_solution(17429413387545831621)
XLA Ops:
  0.6 21.8 %shard_map.67 = (f32[136,128]{1,0:T(8,128)S(1)}, f32[27,16,32]{2,1,0:T(8,128)S(1)}, f32[27,16,32]{2,1,0:T(8,128)S(1)}) custom-call(bf16[136,128]{1,0:T(8,128)(2,1)} %bitcast.7, bf16[136,128]{1,0:T(8,128)(2,1)} %bitcast.8, bf16[3456,128]{1,0:T(8,128)(2,1)} %bitcast.5, bf16[3456,128]{1,0:T(8,128)(2,1)} %bitcast.6), custom_call_target="tpu_custom_call" | custom-call | tf_op jit(solution)/shard_map/pallas_call | solution.py:666
  22.5 0.8 %shard_map.68 = (f32[136,128]{1,0:T(8,128)}, f32[27,16,32]{2,1,0:T(8,128)}, f32[27,16,32]{2,1,0:T(8,128)}) custom-call(f32[136,128]{1,0:T(8,128)S(1)} %get-tuple-element.9.back_ref, f32[27,16,32]{2,1,0:T(8,128)S(1)} %get-tuple-element.10.one_ref, f32[27,16,32]{2,1,0:T(8,128)S(1)} %get-tuple-element.11.two_ref), custom_call_target="tpu_custom_call" | custom-call | tf_op jit(solution)/shard_map/pallas_call | solution.py:732

commit v9 on v8

--- a/solution.py
+++ b/solution.py
@@ -161,14 +161,14 @@
         @pl.when(jnp.logical_not(vert[v]))
         def _():
             rim_in[:, v] = jnp.zeros((2, tmn, cols, C), bf)
-            tip_in[:, v] = jnp.zeros((2, 2, tmn, 8, C), bf)
+            tip_in[:, v] = jnp.zeros((2, 2, tmn, 2, C), bf)
 
     for h in range(2):
 
         @pl.when(jnp.logical_not(side[h]))
         def _():
             edge_in[:, h] = jnp.zeros((2, tmn, rows, C), bf)
-            tip_in[:, :, h] = jnp.zeros((2, 2, tmn, 8, C), bf)
+            tip_in[:, :, h] = jnp.zeros((2, 2, tmn, 2, C), bf)
 
     for which in range(2):
         keep(which).wait()
@@ -179,7 +179,7 @@
             line = flat[which, v * (cells - cols) : v * (cells - cols) + cols, :]
             rim[which, v] = line.astype(bf)
             for h in range(2):
-                tip[which, v, h] = jnp.broadcast_to(line[h * (cols - 1) : h * (cols - 1) + 1], (8, C)).astype(bf)
+                tip[which, v, h] = jnp.broadcast_to(line[h * (cols - 1) : h * (cols - 1) + 1], (2, C)).astype(bf)
 
     def remote(src, dst, send, recv, place):
         return pltpu.make_async_remote_copy(
@@ -699,10 +699,10 @@
             pltpu.VMEM((2, zn, group, channels), bf),
             pltpu.VMEM((2, 2, cols, channels), bf),
             pltpu.VMEM((2, 2, rows, channels), bf),
-            pltpu.VMEM((2, 2, 2, 8, channels), bf),
+            pltpu.VMEM((2, 2, 2, 2, channels), bf),
             pltpu.VMEM((2, 2, tmn, cols, channels), bf),
             pltpu.VMEM((2, 2, tmn, rows, channels), bf),
-            pltpu.VMEM((2, 2, 2, tmn, 8, channels), bf),
+            pltpu.VMEM((2, 2, 2, tmn, 2, channels), bf),
             pltpu.VMEM((2, 3 * cols, channels), bf),
             pltpu.VMEM((2, 3 * rows, channels), bf),
             pltpu.VMEM((2, 3 * cols, channels), bf),

time: 23.5 us -> 23.2 us (0.987)
    pallas_call x1, Pallas kernels: 21.8 us -> 21.6 us  [body(): pl.pallas_call(functools.partial(kernel, dims), out_shape=(pltpu.VMEM((ce...]
where the time goes in v9:
time: 23.2 us; the launch traced here: 23 us
  Pallas kernels  22.4 us (97%)
  between operations  0.64 us (3%)
    pallas_call x1, Pallas kernels, body(): pl.pallas_call(functools.partial(kernel, dims), out_shape=(pltpu.VMEM((ce...  21.6 us
    pallas_call x1, Pallas kernels, body(): pl.pallas_call(finish, out_shape=(jax.ShapeDtypeStruct((cells, channels),...  0.81 us

profile of v9, /device:TPU:0, one launch (start us, length us, event | category | flops | bytes accessed | tf_op | source)
XLA Modules:
  0.0 23.0 jit_solution(10081285167551322541)
XLA Ops:
  0.6 21.6 %shard_map.67 = (f32[136,128]{1,0:T(8,128)S(1)}, f32[27,16,32]{2,1,0:T(8,128)S(1)}, f32[27,16,32]{2,1,0:T(8,128)S(1)}) custom-call(bf16[136,128]{1,0:T(8,128)(2,1)} %bitcast.7, bf16[136,128]{1,0:T(8,128)(2,1)} %bitcast.8, bf16[3456,128]{1,0:T(8,128)(2,1)} %bitcast.5, bf16[3456,128]{1,0:T(8,128)(2,1)} %bitcast.6), custom_call_target="tpu_custom_call" | custom-call | tf_op jit(solution)/shard_map/pallas_call | solution.py:666
  22.2 0.8 %shard_map.68 = (f32[136,128]{1,0:T(8,128)}, f32[27,16,32]{2,1,0:T(8,128)}, f32[27,16,32]{2,1,0:T(8,128)}) custom-call(f32[136,128]{1,0:T(8,128)S(1)} %get-tuple-element.9.back_ref, f32[27,16,32]{2,1,0:T(8,128)S(1)} %get-tuple-element.10.one_ref, f32[27,16,32]{2,1,0:T(8,128)S(1)} %get-tuple-element.11.two_ref), custom_call_target="tpu_custom_call" | custom-call | tf_op jit(solution)/shard_map/pallas_call | solution.py:732

commit v10 on v9

--- a/solution.py
+++ b/solution.py
@@ -451,8 +451,6 @@
         )
         for d in ds:
             conv[partner(d)] = got[(d - ds[0]) * mp : (d - ds[0] + 1) * mp]
-        if ds is not groups[-1]:
-            choose_x(ds)
     for t in range(tmn):
         hidden = conv[t, :cells, 2 * C :]
         for a in range(2):
@@ -550,7 +548,7 @@
 
     scatter(1)
 
-    choose_x(groups[-1])
+    choose_x(range(tmn))
 
     total = None
     for d in range(tmn):

time: 23.2 us -> 23.2 us (level)
  no operation moved by 1% of the time
where the time goes in v10:
time: 23.2 us; the launch traced here: 23 us
  Pallas kernels  22.4 us (97%)
  between operations  0.64 us (3%)
    pallas_call x1, Pallas kernels, body(): pl.pallas_call(functools.partial(kernel, dims), out_shape=(pltpu.VMEM((ce...  21.6 us
    pallas_call x1, Pallas kernels, body(): pl.pallas_call(finish, out_shape=(jax.ShapeDtypeStruct((cells, channels),...  0.81 us

profile of v10, /device:TPU:0, one launch (start us, length us, event | category | flops | bytes accessed | tf_op | source)
XLA Modules:
  0.0 23.0 jit_solution(15226756258002348226)
XLA Ops:
  0.6 21.6 %shard_map.67 = (f32[136,128]{1,0:T(8,128)S(1)}, f32[27,16,32]{2,1,0:T(8,128)S(1)}, f32[27,16,32]{2,1,0:T(8,128)S(1)}) custom-call(bf16[136,128]{1,0:T(8,128)(2,1)} %bitcast.7, bf16[136,128]{1,0:T(8,128)(2,1)} %bitcast.8, bf16[3456,128]{1,0:T(8,128)(2,1)} %bitcast.5, bf16[3456,128]{1,0:T(8,128)(2,1)} %bitcast.6), custom_call_target="tpu_custom_call" | custom-call | tf_op jit(solution)/shard_map/pallas_call | solution.py:664
  22.2 0.8 %shard_map.68 = (f32[136,128]{1,0:T(8,128)}, f32[27,16,32]{2,1,0:T(8,128)}, f32[27,16,32]{2,1,0:T(8,128)}) custom-call(f32[136,128]{1,0:T(8,128)S(1)} %get-tuple-element.9.back_ref, f32[27,16,32]{2,1,0:T(8,128)S(1)} %get-tuple-element.10.one_ref, f32[27,16,32]{2,1,0:T(8,128)S(1)} %get-tuple-element.11.two_ref), custom_call_target="tpu_custom_call" | custom-call | tf_op jit(solution)/shard_map/pallas_call | solution.py:730
